TPU v7x, 128 devices: a whole 4x4x4 slice. The times are simulated.
128 devices in a mesh: cut: 8 (over x_lo, z), cross: 16 (over y, x_hi, core).
Axes of the slice: x: 4 (x_hi: 2, x_lo: 2; x = x_hi * 2 + x_lo), y: 4, z: 4, core: 2. Of those that a mesh axis runs over, the one named last changes fastest.
Arguments:
- warming_above_ambient: float32 [1024, 256, 128], P('cut', 'cross'), may hold values from 0 to 2
- fourier_stability_factor: float32 [1024, 256, 128], P('cut', 'cross'), may hold values from 0.02 to 0.1
- patch_locator: int32 [524288], P(('cut', 'cross')), may hold values from 0 to 524287
- photon_gain_wattage: float32 [524288], P(('cut', 'cross')), may hold values from 0.5 to 4
- on_skin_marker: int32 [524288], P(('cut', 'cross')), may hold values 0 or 1
- grain_placements: float32 [3, 524288], P(None, ('cut', 'cross')), may hold values from -1 to 1
- grain_motion_parts: float32 [3, 524288], P(None, ('cut', 'cross')), may hold values from -3 to 3
- tether_acted_grain: int32 [1048576], P(('cut', 'cross')), may hold values from 0 to 4095
- tether_other_grain: int32 [1048576], P(('cut', 'cross')), may hold values from 0 to 4607
- tether_relaxed_gap: float32 [1048576], P(('cut', 'cross')), may hold values from 0.5 to 1.5
- snapped_marker: int32 [1048576], P(('cut', 'cross')), may hold values 0 or 1
- exported_copies: int32 [32768], P(('cut', 'cross')), may hold values from 0 to 4095
Outputs:
- temperature_new: float32 [1024, 256, 128], P('cut', 'cross')
- positions_new: float32 [3, 524288], P(None, ('cut', 'cross'))
- velocities_new: float32 [3, 524288], P(None, ('cut', 'cross'))
Inputs may be any that keep to these rules, and one draw needn't show every extreme that they name: `patch_locator`: values below 262144 name cells of the particle's own grid block along the cutting direction, the others cells of the next block.
All inputs are finite; a program needn't handle non-finite values. No bound on the sum of `on_skin_marker` or of `snapped_marker` on one device may be relied on, other than what follows from the above.
Results may differ from a plain program's by a relative error of at most 0.000071.
Values sent between devices are 32-bit elements; how exact they have to be, the bound alone decides.
A program may use at most 64 MiB of HBM per device.

v0:
```python
import jax
import jax.numpy as jnp
from jax import lax
from jax.sharding import PartitionSpec as P

STEPS = 3


def shifted(block, axis, distance):
    devices = range(lax.axis_size(axis))
    route = [((i - distance) % len(devices), i) for i in devices]
    return lax.ppermute(block, axis, route)


def with_halo(cells, sides, width):
    for axis, dim in sides:
        count = lax.axis_size(axis)
        head = lax.slice_in_dim(cells, 0, width, axis=dim)
        tail = lax.slice_in_dim(cells, cells.shape[dim] - width, cells.shape[dim], axis=dim)
        cells = jnp.concatenate(
            [
                lax.ppermute(tail, axis, [(i, (i + 1) % count) for i in range(count)]),
                cells,
                lax.ppermute(head, axis, [((i + 1) % count, i) for i in range(count)]),
            ],
            axis=dim,
        )
    return cells


def conduct(grain_warmth_reading):
    return 0.5 + 1.0 / (1.0 + grain_warmth_reading * grain_warmth_reading)


def advance(temp_pad, kappa_pad, thermal_input):
    temp_full = jnp.pad(temp_pad, ((0, 0), (0, 0), (1, 1)))
    kappa_full = jnp.pad(kappa_pad, ((0, 0), (0, 0), (1, 1)))
    conduct_full = kappa_full * conduct(temp_full)
    size_a = temp_full.shape[0] - 2
    size_b = temp_full.shape[1] - 2
    size_c = temp_full.shape[2] - 2
    center = temp_full[1 : 1 + size_a, 1 : 1 + size_b, 1 : 1 + size_c]
    middle = conduct_full[1 : 1 + size_a, 1 : 1 + size_b, 1 : 1 + size_c]
    change = jnp.zeros_like(center)
    for first, second, third in ((2, 1, 1), (0, 1, 1), (1, 2, 1), (1, 0, 1), (1, 1, 2), (1, 1, 0)):
        beside = temp_full[first : first + size_a, second : second + size_b, third : third + size_c]
        beside_c = conduct_full[
            first : first + size_a, second : second + size_b, third : third + size_c
        ]
        change = change + 0.5 * (middle + beside_c) * (beside - center)
    return center + (change + thermal_input)


def clear_rim(field, axis_dim, width):
    extent = field.shape[axis_dim]
    place = lax.broadcasted_iota(jnp.int32, field.shape, axis_dim)
    position = lax.axis_index("cross")
    final = lax.axis_size("cross") - 1
    drop = (place < width) & (position == 0) | (place >= extent - width) & (position == final)
    return jnp.where(drop, jnp.zeros_like(field), field)


def table_rows(table):
    channels = table.shape[0]
    columns = table.shape[1]
    padded_cols = -(-columns // 128) * 128
    high_count = padded_cols // 128
    return (
        table.reshape(channels, high_count, 128)
        .transpose(1, 0, 2)
        .reshape(high_count, channels * 128)
    )


def pick_columns(table, where_from):
    channels = table.shape[0]
    stacked_rows = table_rows(table)
    high_count = stacked_rows.shape[0]
    total_rows = where_from.shape[0]
    block_rows = min(1024, total_rows)

    def pick_block(idx_block):
        high_part = idx_block // 128
        low_part = idx_block % 128
        row_hot = (
            high_part[:, None] == lax.broadcasted_iota(jnp.int32, (1, high_count), 1)
        ).astype(jnp.float32)
        picked = jnp.dot(
            row_hot,
            stacked_rows,
            precision=lax.Precision.HIGHEST,
            preferred_element_type=jnp.float32,
        )
        picked = picked.reshape(idx_block.shape[0], channels, 128)
        lane_hot = (low_part[:, None] == lax.broadcasted_iota(jnp.int32, (1, 128), 1)).astype(
            jnp.float32
        )
        return jnp.sum(picked * lane_hot[:, None, :], axis=2)

    result = lax.map(pick_block, where_from.reshape(total_rows // block_rows, block_rows))
    return result.reshape(total_rows, channels).T


def add_columns(values, where_to, columns):
    channels = values.shape[0]
    total_rows = where_to.shape[0]
    block_rows = min(1024, total_rows)
    padded_cols = -(-columns // 128) * 128
    high_count = padded_cols // 128
    value_blocks = values.T.reshape(total_rows // block_rows, block_rows, channels)
    index_blocks = where_to.reshape(total_rows // block_rows, block_rows)

    def add_block(carried, pieces):
        value_block, idx_block = pieces
        high_part = idx_block // 128
        low_part = idx_block % 128
        row_hot = (
            high_part[:, None] == lax.broadcasted_iota(jnp.int32, (1, high_count), 1)
        ).astype(jnp.float32)
        lane_hot = (low_part[:, None] == lax.broadcasted_iota(jnp.int32, (1, 128), 1)).astype(
            jnp.float32
        )
        spread = (value_block[:, :, None] * lane_hot[:, None, :]).reshape(
            idx_block.shape[0], channels * 128
        )
        summed = lax.dot_general(
            row_hot,
            spread,
            (((0,), (0,)), ((), ())),
            precision=lax.Precision.HIGHEST,
            preferred_element_type=jnp.float32,
        )
        return (carried + summed, None)

    start_total = jnp.zeros((high_count, channels * 128), jnp.float32)
    totals, unused = lax.scan(add_block, start_total, (value_blocks, index_blocks))
    return (
        totals.reshape(high_count, channels, 128).transpose(1, 0, 2).reshape(channels, padded_cols)
    )


def per_device(
    warming_above_ambient,
    fourier_stability_factor,
    patch_locator,
    photon_gain_wattage,
    on_skin_marker,
    grain_placements,
    grain_motion_parts,
    tether_acted_grain,
    tether_other_grain,
    tether_relaxed_gap,
    snapped_marker,
    exported_copies,
):
    groups = lax.axis_size("cross")
    count = patch_locator.shape[0]
    capacity = count // groups
    structured_patch = (
        warming_above_ambient.shape[0]
        * warming_above_ambient.shape[1]
        * warming_above_ambient.shape[2]
    )
    energy_current = on_skin_marker.astype(jnp.float32) * photon_gain_wattage * 0.5
    got_cells, got_flux = (
        lax.all_to_all(
            patch_locator.reshape(groups, capacity),
            "cross",
            split_axis=0,
            concat_axis=0,
            tiled=True,
        ),
        lax.all_to_all(
            energy_current.reshape(groups, capacity),
            "cross",
            split_axis=0,
            concat_axis=0,
            tiled=True,
        ),
    )
    got_cells = got_cells.reshape(-1)
    got_flux = got_flux.reshape(-1)
    volume_tile_layout = add_columns(got_flux[None, :], got_cells, 2 * structured_patch)[0]
    arriving_copies = shifted(
        volume_tile_layout[structured_patch:].reshape(warming_above_ambient.shape), "cut", 1
    )
    thermal_input = (
        volume_tile_layout[:structured_patch].reshape(warming_above_ambient.shape) + arriving_copies
    )
    grain_warmth_reading = warming_above_ambient
    kappa_pad = clear_rim(with_halo(fourier_stability_factor, (("cut", 0), ("cross", 1)), 1), 1, 1)
    for substep in range(STEPS):
        temp_pad = clear_rim(with_halo(grain_warmth_reading, (("cut", 0), ("cross", 1)), 1), 1, 1)
        grain_warmth_reading = advance(temp_pad, kappa_pad, thermal_input)
    temp_flat = grain_warmth_reading.reshape(1, -1)
    ahead = shifted(grain_warmth_reading, "cut", -1)
    whole = jnp.concatenate([temp_flat, ahead.reshape(1, -1)], axis=1)
    looked = pick_columns(whole, got_cells)[0]
    particle_temp = lax.all_to_all(
        looked.reshape(groups, capacity), "cross", split_axis=0, concat_axis=0, tiled=True
    ).reshape(-1)
    state = jnp.concatenate([grain_placements, particle_temp[None, :]], axis=0)
    ghost_count = exported_copies.shape[0]
    ghost_data = pick_columns(state, exported_copies)
    ghost_wide = with_halo(ghost_data, (("cut", 1),), ghost_count)
    extended = jnp.concatenate(
        [state, ghost_wide[:, :ghost_count], ghost_wide[:, 2 * ghost_count :]], axis=1
    )
    first_state = pick_columns(state, tether_acted_grain)
    second_state = pick_columns(extended, tether_other_grain)
    delta = second_state[:3] - first_state[:3]
    dist = jnp.sqrt(jnp.sum(delta * delta, axis=0))
    hot = tether_relaxed_gap * (1.0 + 0.2 * (0.5 * (first_state[3] + second_state[3])))
    scale = (1.0 - snapped_marker.astype(jnp.float32)) * (dist - hot) / jnp.maximum(dist, 0.3)
    force = add_columns(scale * delta, tether_acted_grain, count)
    velocities_new = grain_motion_parts + 0.5 * force
    positions_new = grain_placements + 0.5 * velocities_new
    return (grain_warmth_reading, positions_new, velocities_new)


def solution(mesh):
    return jax.shard_map(
        per_device,
        mesh=mesh,
        in_specs=(
            P("cut", "cross", None),
            P("cut", "cross", None),
            P(("cut", "cross")),
            P(("cut", "cross")),
            P(("cut", "cross")),
            P(None, ("cut", "cross")),
            P(None, ("cut", "cross")),
            P(("cut", "cross")),
            P(("cut", "cross")),
            P(("cut", "cross")),
            P(("cut", "cross")),
            P(("cut", "cross")),
        ),
        out_specs=(P("cut", "cross", None), P(None, ("cut", "cross")), P(None, ("cut", "cross"))),
        check_vma=False,
    )
```

profile of v0, /device:TPU:0, one launch (start us, length us, event | category | flops | bytes accessed | tf_op | source)
XLA Modules:
  0.0 295.9 jit_solution(1957431094238829777)
XLA Ops:
  1.3 2.0 collective-permute-start
  3.4 3.0 %collective-permute-start.1 = (f32[1,16,128]{2,1,0:T(8,128)S(1)}, f32[1,16,128]{2,1,0:T(8,128)S(1)}, u32[]{:S(2)}, u32[]{:S(2)}) collective-permute-start(f32[1,16,128]{2,1,0:T(8,128)S(1)} %get-tuple-element.423), channel_id=1, source_target_pairs={{16,0},{32,16},{48,32},{64,48},{80,64},{96,80},{112,96},{0,112},{1... | collective-permute-start | bytes 24584 | tf_op jit(solution)/shard_map/ppermute | solution.py:24
  7.1 4.1 %collective-permute-start.5 = (f32[1,16,128]{2,1,0:T(8,128)S(1)}, f32[1,16,128]{2,1,0:T(8,128)S(1)}, u32[]{:S(2)}, u32[]{:S(2)}) collective-permute-start(f32[1,16,128]{2,1,0:T(8,128)S(1)} %get-tuple-element.421), channel_id=1, source_target_pairs={{16,0},{32,16},{48,32},{64,48},{80,64},{96,80},{112,96},{0,112},{1... | collective-permute-start | bytes 24584 | tf_op jit(solution)/shard_map/ppermute | solution.py:24
  11.3 6.7 %all-to-all-start = ((s32[16,1,256]{2,1,0:T(1,128)}), s32[16,1,256]{2,1,0:T(1,128)S(1)}, u32[]{:S(2)}, u32[]{:S(2)}) async-start(s32[16,1,256]{2,1,0:T(1,128)} %bitcast.137), calls=%async_computation | async-start | bytes 32768 | tf_op jit(solution)/shard_map/all_to_all | solution.py:166
  18.0 1.3 multiply_multiply_fusion
  19.4 1.3 constant_dynamic-update-slice_fusion.2
  21.3 5.0 %collective-permute-start.3 = (f32[130,1,128]{2,0,1:T(8,128)S(1)}, f32[130,1,128]{2,0,1:T(8,128)S(1)}, u32[]{:S(2)}, u32[]{:S(2)}) collective-permute-start(f32[130,1,128]{2,0,1:T(8,128)S(1)} %copy.42), channel_id=1, source_target_pairs={{1,0},{2,1},{3,2},{4,3},{5,4},{6,5},{7,6},{8,7},{9,8},{10,9},{11,1... | collective-permute-start | bytes 199688 | tf_op jit(solution)/shard_map/ppermute | solution.py:24
  26.3 5.1 %all-to-all-start.1 = ((f32[16,1,256]{2,1,0:T(1,128)}), f32[16,1,256]{2,1,0:T(1,128)S(1)}, u32[]{:S(2)}, u32[]{:S(2)}) async-start(f32[16,1,256]{2,1,0:T(1,128)} %bitcast.9), calls=%async_computation.1 | async-start | bytes 32768 | tf_op jit(solution)/shard_map/all_to_all | solution.py:173
  31.4 1.3 constant_dynamic-update-slice_fusion.5
  32.8 6.2 %all-to-all-done.1 = f32[16,1,256]{2,1,0:T(1,128)S(1)} async-done(((f32[16,1,256]{2,1,0:T(1,128)}), f32[16,1,256]{2,1,0:T(1,128)S(1)}, u32[]{:S(2)}, u32[]{:S(2)}) %all-to-all-start.1) | async-done | bytes 16416 | tf_op jit(solution)/shard_map/all_to_all | solution.py:173
  39.0 59.0 %while.69 = (s32[]{:T(128)}, f32[4096,128]{1,0:T(8,128)S(1)}, s32[4,1024]{1,0:T(4,128)S(1)}, f32[4,1024,1]{1,2,0:T(1,128)S(1)}, s32[]{:T(128)}, /*index=5*/s32[]{:T(128)}) while((s32[]{:T(128)}, f32[4096,128]{1,0:T(8,128)S(1)}, s32[4,1024]{1,0:T(4,128)S(1)}, f32[4,1024,1]{1,2,0:T(1,128)S(1)}, s32[]{:T(128)}, ...), condition=%wide.region_1.2_spmd.clone, body=%wide.region_0.1_spmd.clone.sunk | while | flops 6447975424 | bytes 4235351 | solution.py:136
  39.2 14.5 %fusion.143 = f32[4096,128]{1,0:T(8,128)S(1)} fusion(s32[1024]{0:T(1024)S(1)} %get-tuple-element.568, f32[4096,128]{1,0:T(8,128)S(1)} %get-tuple-element.583, pred[]{:T(512)S(6)} %compare.73, f32[1024]{0:T(1024)S(1)} %bitcast.134, s32[1024]{0:T(1024)S(1)} %get-tuple-element.569), kind=kOutput, calls=%fused_computation.51.clone.1 | convolution fusion | flops 6447955968 | bytes 4206593 | tf_op jit(solution)/shard_map/while/body/eval_jaxpr/dot_general | solution.py:126
  53.8 14.5 %fusion.143 = f32[4096,128]{1,0:T(8,128)S(1)} fusion(s32[1024]{0:T(1024)S(1)} %get-tuple-element.568, f32[4096,128]{1,0:T(8,128)S(1)} %get-tuple-element.583, pred[]{:T(512)S(6)} %compare.73, f32[1024]{0:T(1024)S(1)} %bitcast.134, s32[1024]{0:T(1024)S(1)} %get-tuple-element.569), kind=kOutput, calls=%fused_computation.51.clone.1 | convolution fusion | flops 6447955968 | bytes 4206593 | tf_op jit(solution)/shard_map/while/body/eval_jaxpr/dot_general | solution.py:126
  68.4 14.5 %fusion.143 = f32[4096,128]{1,0:T(8,128)S(1)} fusion(s32[1024]{0:T(1024)S(1)} %get-tuple-element.568, f32[4096,128]{1,0:T(8,128)S(1)} %get-tuple-element.583, pred[]{:T(512)S(6)} %compare.73, f32[1024]{0:T(1024)S(1)} %bitcast.134, s32[1024]{0:T(1024)S(1)} %get-tuple-element.569), kind=kOutput, calls=%fused_computation.51.clone.1 | convolution fusion | flops 6447955968 | bytes 4206593 | tf_op jit(solution)/shard_map/while/body/eval_jaxpr/dot_general | solution.py:126
  83.1 14.5 %fusion.143 = f32[4096,128]{1,0:T(8,128)S(1)} fusion(s32[1024]{0:T(1024)S(1)} %get-tuple-element.568, f32[4096,128]{1,0:T(8,128)S(1)} %get-tuple-element.583, pred[]{:T(512)S(6)} %compare.73, f32[1024]{0:T(1024)S(1)} %bitcast.134, s32[1024]{0:T(1024)S(1)} %get-tuple-element.569), kind=kOutput, calls=%fused_computation.51.clone.1 | convolution fusion | flops 6447955968 | bytes 4206593 | tf_op jit(solution)/shard_map/while/body/eval_jaxpr/dot_general | solution.py:126
  98.6 5.2 %collective-permute-start.7 = (f32[130,1,128]{2,0,1:T(8,128)S(1)}, f32[130,1,128]{2,0,1:T(8,128)S(1)}, u32[]{:S(2)}, u32[]{:S(2)}) collective-permute-start(f32[130,1,128]{2,0,1:T(8,128)S(1)} %copy.46), channel_id=1, source_target_pairs={{1,0},{2,1},{3,2},{4,3},{5,4},{6,5},{7,6},{8,7},{9,8},{10,9},{11,1... | collective-permute-start | bytes 199688 | tf_op jit(solution)/shard_map/ppermute | solution.py:24
  104.0 1.9 collective-permute-done.6
  106.7 1.7 pad_multiply_fusion.5
  108.4 17.8 %collective-permute-done.8 = f32[128,16,128]{2,1,0:T(8,128)S(1)} collective-permute-done((f32[128,16,128]{2,1,0:T(8,128)S(1)}, f32[128,16,128]{2,1,0:T(8,128)S(1)}, u32[]{:S(2)}, u32[]{:S(2)}) %collective-permute-start.8) | collective-permute-done | bytes 1048608 | tf_op jit(solution)/shard_map/ppermute | solution.py:12
  126.3 2.9 fusion.47
  129.2 3.1 %collective-permute-start.10 = (f32[1,16,128]{2,1,0:T(8,128)S(1)}, f32[1,16,128]{2,1,0:T(8,128)S(1)}, u32[]{:S(2)}, u32[]{:S(2)}) collective-permute-start(f32[1,16,128]{2,1,0:T(8,128)S(1)} %get-tuple-element.420), channel_id=1, source_target_pairs={{16,0},{32,16},{48,32},{64,48},{80,64},{96,80},{112,96},{0,112},{1... | collective-permute-start | bytes 24584 | tf_op jit(solution)/shard_map/ppermute | solution.py:24
  132.3 1.4 collective-permute-done.10
  133.6 4.4 %collective-permute-done.9 = f32[1,16,128]{2,1,0:T(8,128)S(1)} collective-permute-done((f32[1,16,128]{2,1,0:T(8,128)S(1)}, f32[1,16,128]{2,1,0:T(8,128)S(1)}, u32[]{:S(2)}, u32[]{:S(2)}) %collective-permute-start.9) | collective-permute-done | bytes 8224 | tf_op jit(solution)/shard_map/ppermute | solution.py:22
  138.2 5.3 %collective-permute-start.12 = (f32[130,1,128]{2,0,1:T(8,128)S(1)}, f32[130,1,128]{2,0,1:T(8,128)S(1)}, u32[]{:S(2)}, u32[]{:S(2)}) collective-permute-start(f32[130,1,128]{2,0,1:T(8,128)S(1)} %copy.51), channel_id=1, source_target_pairs={{1,0},{2,1},{3,2},{4,3},{5,4},{6,5},{7,6},{8,7},{9,8},{10,9},{11,1... | collective-permute-start | bytes 199688 | tf_op jit(solution)/shard_map/ppermute | solution.py:24
  143.6 2.0 collective-permute-done.11
  146.0 1.7 pad_multiply_fusion.4
  147.8 2.9 fusion.55
  150.8 4.1 %collective-permute-start.14 = (f32[1,16,128]{2,1,0:T(8,128)S(1)}, f32[1,16,128]{2,1,0:T(8,128)S(1)}, u32[]{:S(2)}, u32[]{:S(2)}) collective-permute-start(f32[1,16,128]{2,1,0:T(8,128)S(1)} %get-tuple-element.418), channel_id=1, source_target_pairs={{16,0},{32,16},{48,32},{64,48},{80,64},{96,80},{112,96},{0,112},{1... | collective-permute-start | bytes 24584 | tf_op jit(solution)/shard_map/ppermute | solution.py:24
  154.9 1.6 collective-permute-done.13
  157.0 5.0 %collective-permute-start.16 = (f32[130,1,128]{2,0,1:T(8,128)S(1)}, f32[130,1,128]{2,0,1:T(8,128)S(1)}, u32[]{:S(2)}, u32[]{:S(2)}) collective-permute-start(f32[130,1,128]{2,0,1:T(8,128)S(1)} %copy.55), channel_id=1, source_target_pairs={{1,0},{2,1},{3,2},{4,3},{5,4},{6,5},{7,6},{8,7},{9,8},{10,9},{11,1... | collective-permute-start | bytes 199688 | tf_op jit(solution)/shard_map/ppermute | solution.py:24
  162.1 2.5 collective-permute-done.15
  165.0 1.7 pad_multiply_fusion.3
  166.7 2.9 fusion.63
  169.6 4.3 %collective-permute-start.17 = (f32[128,16,128]{2,1,0:T(8,128)S(1)}, f32[128,16,128]{2,1,0:T(8,128)S(1)}, u32[]{:S(2)}, u32[]{:S(2)}) collective-permute-start(f32[128,16,128]{2,1,0:T(8,128)S(1)} %fusion.63), channel_id=1, source_target_pairs={{16,0},{32,16},{48,32},{64,48},{80,64},{96,80},{112,96},{0,112},{1... | collective-permute-start | bytes 3145736 | tf_op jit(solution)/shard_map/ppermute | solution.py:12
  173.9 21.0 %collective-permute-done.17 = f32[128,16,128]{2,1,0:T(8,128)S(1)} collective-permute-done((f32[128,16,128]{2,1,0:T(8,128)S(1)}, f32[128,16,128]{2,1,0:T(8,128)S(1)}, u32[]{:S(2)}, u32[]{:S(2)}) %collective-permute-start.17) | collective-permute-done | bytes 1048608 | tf_op jit(solution)/shard_map/ppermute | solution.py:12
  195.9 7.6 %pad_maximum_fusion = f32[1,524288]{1,0:T(1,128)S(1)} fusion(f32[1,262144]{1,0:T(1,128)} %bitcast.120, f32[1,262144]{1,0:T(1,128)S(1)} %bitcast.107), kind=kLoop, calls=%fused_computation.106 | loop fusion | flops 524288 | bytes 4194304 | tf_op jit(solution)/shard_map/concatenate | solution.py:197
  203.6 40.3 %while.66 = (s32[]{:T(128)}, f32[4,1024,1]{1,2,0:T(1,128)}, s32[4,1024]{1,0:T(4,128)S(1)}, f32[4096,128]{1,0:T(8,128)S(1)}, s32[]{:T(128)}) while((s32[]{:T(128)}, f32[4,1024,1]{1,2,0:T(1,128)}, s32[4,1024]{1,0:T(4,128)S(1)}, f32[4096,128]{1,0:T(8,128)S(1)}, s32[]{:T(128)}) %tuple.179), condition=%wide.region_4.5_spmd, body=%wide.region_2.4_spmd.sunk | while | flops 6447056896 | bytes 2138689 | solution.py:100
  203.7 9.4 %fusion.137 = f32[1024]{0:T(1024)S(1)} fusion(f32[4096,128]{1,0:T(8,128)S(1)} %get-tuple-element.607, s32[1024]{0:T(1024)S(1)} %get-tuple-element.550, s32[1024]{0:T(1024)S(1)} %get-tuple-element.551), kind=kOutput, calls=%fused_computation.4.clone.1 | convolution fusion | flops 6447037440 | bytes 2109440 | tf_op jit(solution)/shard_map/while/body/eval_jaxpr/dot_general | solution.py:88
  213.7 9.4 %fusion.137 = f32[1024]{0:T(1024)S(1)} fusion(f32[4096,128]{1,0:T(8,128)S(1)} %get-tuple-element.607, s32[1024]{0:T(1024)S(1)} %get-tuple-element.550, s32[1024]{0:T(1024)S(1)} %get-tuple-element.551), kind=kOutput, calls=%fused_computation.4.clone.1 | convolution fusion | flops 6447037440 | bytes 2109440 | tf_op jit(solution)/shard_map/while/body/eval_jaxpr/dot_general | solution.py:88
  223.8 9.4 %fusion.137 = f32[1024]{0:T(1024)S(1)} fusion(f32[4096,128]{1,0:T(8,128)S(1)} %get-tuple-element.607, s32[1024]{0:T(1024)S(1)} %get-tuple-element.550, s32[1024]{0:T(1024)S(1)} %get-tuple-element.551), kind=kOutput, calls=%fused_computation.4.clone.1 | convolution fusion | flops 6447037440 | bytes 2109440 | tf_op jit(solution)/shard_map/while/body/eval_jaxpr/dot_general | solution.py:88
  233.9 9.4 %fusion.137 = f32[1024]{0:T(1024)S(1)} fusion(f32[4096,128]{1,0:T(8,128)S(1)} %get-tuple-element.607, s32[1024]{0:T(1024)S(1)} %get-tuple-element.550, s32[1024]{0:T(1024)S(1)} %get-tuple-element.551), kind=kOutput, calls=%fused_computation.4.clone.1 | convolution fusion | flops 6447037440 | bytes 2109440 | tf_op jit(solution)/shard_map/while/body/eval_jaxpr/dot_general | solution.py:88
  244.0 3.5 %all-to-all-start.2 = ((f32[16,1,256]{2,1,0:T(1,128)}), f32[16,1,256]{2,1,0:T(1,128)S(1)}, u32[]{:S(2)}, u32[]{:S(2)}) async-start(f32[16,1,256]{2,1,0:T(1,128)} %bitcast.16), calls=%async_computation.2 | async-start | bytes 32768 | tf_op jit(solution)/shard_map/all_to_all | solution.py:199
  247.5 7.4 %all-to-all-done.2 = f32[16,1,256]{2,1,0:T(1,128)S(1)} async-done(((f32[16,1,256]{2,1,0:T(1,128)}), f32[16,1,256]{2,1,0:T(1,128)S(1)}, u32[]{:S(2)}, u32[]{:S(2)}) %all-to-all-start.2) | async-done | bytes 16416 | tf_op jit(solution)/shard_map/all_to_all | solution.py:199
  255.6 4.9 %collective-permute-start.19 = (f32[4,256]{1,0:T(4,128)S(1)}, f32[4,256]{1,0:T(4,128)S(1)}, u32[]{:S(2)}, u32[]{:S(2)}) collective-permute-start(f32[4,256]{1,0:T(4,128)S(1)} %bitcast.139), channel_id=1, source_target_pairs={{16,0},{32,16},{48,32},{64,48},{80,64},{96,80},{112,96},{0,112},{1... | collective-permute-start | bytes 12296 | tf_op jit(solution)/shard_map/ppermute | solution.py:24
  260.5 11.2 %while.68 = (s32[]{:T(128)}, f32[8,1024,4]{1,2,0:T(4,128)S(1)}, s32[8,1024]{1,0:T(8,128)S(1)}, f32[32,512]{1,0:T(8,128)S(1)}, s32[]{:T(128)}) while((s32[]{:T(128)}, f32[8,1024,4]{1,2,0:T(4,128)S(1)}, s32[8,1024]{1,0:T(8,128)S(1)}, f32[32,512]{1,0:T(8,128)S(1)}, s32[]{:T(128)}) %tuple.176), condition=%wide.region_11.12_spmd, body=%wide.region_9.11_spmd.sunk | while | flops 202685440 | bytes 1192005 | solution.py:100
  271.9 11.3 %while.67 = (s32[]{:T(128)}, f32[8,1024,4]{1,2,0:T(4,128)S(1)}, s32[8,1024]{1,0:T(8,128)S(1)}, f32[36,512]{1,0:T(8,128)S(1)}, s32[]{:T(128)}) while((s32[]{:T(128)}, f32[8,1024,4]{1,2,0:T(4,128)S(1)}, s32[8,1024]{1,0:T(8,128)S(1)}, f32[36,512]{1,0:T(8,128)S(1)}, s32[]{:T(128)}) %tuple.175), condition=%wide.region_8.9_spmd, body=%wide.region_6.8_spmd.sunk | while | flops 227855360 | bytes 1200197 | solution.py:100
  272.0 1.3 multiply_reduce_fusion.5
  283.5 11.4 %while.70 = (s32[]{:T(128)}, f32[32,384]{1,0:T(8,128)S(1)}, s32[8,1024]{1,0:T(8,128)S(1)}, f32[8,1024,3]{1,2,0:T(4,128)S(1)}, s32[]{:T(128)}, /*index=5*/s32[]{:T(128)}) while((s32[]{:T(128)}, f32[32,384]{1,0:T(8,128)S(1)}, s32[8,1024]{1,0:T(8,128)S(1)}, f32[8,1024,3]{1,2,0:T(4,128)S(1)}, s32[]{:T(128)}, ...), condition=%wide.region_14.15_spmd.clone, body=%wide.region_13.14_spmd.clone.sunk | while | flops 151759872 | bytes 4358231 | solution.py:136
  (254 shorter events, 42.2 us)
Async XLA Ops:
  1.3 18.0 %collective-permute-start = (f32[1,16,128]{2,1,0:T(8,128)S(1)}, f32[1,16,128]{2,1,0:T(8,128)S(1)}, u32[]{:S(2)}, u32[]{:S(2)}) collective-permute-start(f32[1,16,128]{2,1,0:T(8,128)S(1)} %get-tuple-element.424), channel_id=1, source_target_pairs={{0,16},{16,32},{32,48},{48,64},{64,80},{80,96},{96,112},{112,0},{1... | collective-permute-start | bytes 24584 | tf_op jit(solution)/shard_map/ppermute | solution.py:22
  3.4 17.3 %collective-permute-start.1 = (f32[1,16,128]{2,1,0:T(8,128)S(1)}, f32[1,16,128]{2,1,0:T(8,128)S(1)}, u32[]{:S(2)}, u32[]{:S(2)}) collective-permute-start(f32[1,16,128]{2,1,0:T(8,128)S(1)} %get-tuple-element.423), channel_id=1, source_target_pairs={{16,0},{32,16},{48,32},{64,48},{80,64},{96,80},{112,96},{0,112},{1... | collective-permute-start | bytes 24584 | tf_op jit(solution)/shard_map/ppermute | solution.py:24
  7.1 19.1 %collective-permute-start.4 = (f32[1,16,128]{2,1,0:T(8,128)S(1)}, f32[1,16,128]{2,1,0:T(8,128)S(1)}, u32[]{:S(2)}, u32[]{:S(2)}) collective-permute-start(f32[1,16,128]{2,1,0:T(8,128)S(1)} %get-tuple-element.422), channel_id=1, source_target_pairs={{0,16},{16,32},{32,48},{48,64},{64,80},{80,96},{96,112},{112,0},{1... | collective-permute-start | bytes 24584 | tf_op jit(solution)/shard_map/ppermute | solution.py:22
  7.1 91.1 %collective-permute-start.5 = (f32[1,16,128]{2,1,0:T(8,128)S(1)}, f32[1,16,128]{2,1,0:T(8,128)S(1)}, u32[]{:S(2)}, u32[]{:S(2)}) collective-permute-start(f32[1,16,128]{2,1,0:T(8,128)S(1)} %get-tuple-element.421), channel_id=1, source_target_pairs={{16,0},{32,16},{48,32},{64,48},{80,64},{96,80},{112,96},{0,112},{1... | collective-permute-start | bytes 24584 | tf_op jit(solution)/shard_map/ppermute | solution.py:24
  11.3 15.0 %all-to-all-start = ((s32[16,1,256]{2,1,0:T(1,128)}), s32[16,1,256]{2,1,0:T(1,128)S(1)}, u32[]{:S(2)}, u32[]{:S(2)}) async-start(s32[16,1,256]{2,1,0:T(1,128)} %bitcast.137), calls=%async_computation | async-start | bytes 32768 | tf_op jit(solution)/shard_map/all_to_all | solution.py:166
  20.7 5.6 %copy-start.1 = (f32[130,16,128]{2,1,0:T(8,128)}, f32[130,16,128]{2,1,0:T(8,128)S(1)}, u32[]{:S(2)}) copy-start(f32[130,16,128]{2,1,0:T(8,128)S(1)} %constant_dynamic-update-slice_fusion.1) | copy-start | bytes 3194884
  20.8 83.0 %collective-permute-start.2 = (f32[130,1,128]{2,0,1:T(8,128)S(1)}, f32[130,1,128]{2,0,1:T(8,128)S(1)}, u32[]{:S(2)}, u32[]{:S(2)}) collective-permute-start(f32[130,1,128]{2,0,1:T(8,128)S(1)} %copy.41), channel_id=1, source_target_pairs={{0,1},{1,2},{2,3},{3,4},{4,5},{5,6},{6,7},{7,8},{8,9},{9,10},{10,1... | collective-permute-start | bytes 199688 | tf_op jit(solution)/shard_map/ppermute | solution.py:22
  21.3 82.6 %collective-permute-start.3 = (f32[130,1,128]{2,0,1:T(8,128)S(1)}, f32[130,1,128]{2,0,1:T(8,128)S(1)}, u32[]{:S(2)}, u32[]{:S(2)}) collective-permute-start(f32[130,1,128]{2,0,1:T(8,128)S(1)} %copy.42), channel_id=1, source_target_pairs={{1,0},{2,1},{3,2},{4,3},{5,4},{6,5},{7,6},{8,7},{9,8},{10,9},{11,1... | collective-permute-start | bytes 199688 | tf_op jit(solution)/shard_map/ppermute | solution.py:24
  26.3 12.7 %all-to-all-start.1 = ((f32[16,1,256]{2,1,0:T(1,128)}), f32[16,1,256]{2,1,0:T(1,128)S(1)}, u32[]{:S(2)}, u32[]{:S(2)}) async-start(f32[16,1,256]{2,1,0:T(1,128)} %bitcast.9), calls=%async_computation.1 | async-start | bytes 32768 | tf_op jit(solution)/shard_map/all_to_all | solution.py:173
  98.2 7.9 %copy-start.2 = (f32[130,16,128]{2,1,0:T(8,128)S(1)}, f32[130,16,128]{2,1,0:T(8,128)}, u32[]{:S(2)}) copy-start(f32[130,16,128]{2,1,0:T(8,128)} %copy-done.1) | copy-start | bytes 3194884
  98.2 28.1 %collective-permute-start.8 = (f32[128,16,128]{2,1,0:T(8,128)S(1)}, f32[128,16,128]{2,1,0:T(8,128)S(1)}, u32[]{:S(2)}, u32[]{:S(2)}) collective-permute-start(f32[128,16,128]{2,1,0:T(8,128)S(1)} %bitcast.119), channel_id=1, source_target_pairs={{112,0},{0,16},{16,32},{32,48},{48,64},{64,80},{80,96},{96,112},{1... | collective-permute-start | bytes 3145736 | tf_op jit(solution)/shard_map/ppermute | solution.py:12
  98.4 7.5 %collective-permute-start.6 = (f32[130,1,128]{2,0,1:T(8,128)S(1)}, f32[130,1,128]{2,0,1:T(8,128)S(1)}, u32[]{:S(2)}, u32[]{:S(2)}) collective-permute-start(f32[130,1,128]{2,0,1:T(8,128)S(1)} %copy.45), channel_id=1, source_target_pairs={{0,1},{1,2},{2,3},{3,4},{4,5},{5,6},{6,7},{7,8},{8,9},{9,10},{10,1... | collective-permute-start | bytes 199688 | tf_op jit(solution)/shard_map/ppermute | solution.py:22
  98.6 7.4 %collective-permute-start.7 = (f32[130,1,128]{2,0,1:T(8,128)S(1)}, f32[130,1,128]{2,0,1:T(8,128)S(1)}, u32[]{:S(2)}, u32[]{:S(2)}) collective-permute-start(f32[130,1,128]{2,0,1:T(8,128)S(1)} %copy.46), channel_id=1, source_target_pairs={{1,0},{2,1},{3,2},{4,3},{5,4},{6,5},{7,6},{8,7},{9,8},{10,9},{11,1... | collective-permute-start | bytes 199688 | tf_op jit(solution)/shard_map/ppermute | solution.py:24
  129.2 4.4 %collective-permute-start.10 = (f32[1,16,128]{2,1,0:T(8,128)S(1)}, f32[1,16,128]{2,1,0:T(8,128)S(1)}, u32[]{:S(2)}, u32[]{:S(2)}) collective-permute-start(f32[1,16,128]{2,1,0:T(8,128)S(1)} %get-tuple-element.420), channel_id=1, source_target_pairs={{16,0},{32,16},{48,32},{64,48},{80,64},{96,80},{112,96},{0,112},{1... | collective-permute-start | bytes 24584 | tf_op jit(solution)/shard_map/ppermute | solution.py:24
  132.3 5.8 %collective-permute-start.9 = (f32[1,16,128]{2,1,0:T(8,128)S(1)}, f32[1,16,128]{2,1,0:T(8,128)S(1)}, u32[]{:S(2)}, u32[]{:S(2)}) collective-permute-start(f32[1,16,128]{2,1,0:T(8,128)S(1)} %get-tuple-element.419), channel_id=1, source_target_pairs={{0,16},{16,32},{32,48},{48,64},{64,80},{80,96},{96,112},{112,0},{1... | collective-permute-start | bytes 24584 | tf_op jit(solution)/shard_map/ppermute | solution.py:22
  138.1 7.4 %collective-permute-start.11 = (f32[130,1,128]{2,0,1:T(8,128)S(1)}, f32[130,1,128]{2,0,1:T(8,128)S(1)}, u32[]{:S(2)}, u32[]{:S(2)}) collective-permute-start(f32[130,1,128]{2,0,1:T(8,128)S(1)} %copy.50), channel_id=1, source_target_pairs={{0,1},{1,2},{2,3},{3,4},{4,5},{5,6},{6,7},{7,8},{8,9},{9,10},{10,1... | collective-permute-start | bytes 199688 | tf_op jit(solution)/shard_map/ppermute | solution.py:22
  138.2 7.4 %collective-permute-start.12 = (f32[130,1,128]{2,0,1:T(8,128)S(1)}, f32[130,1,128]{2,0,1:T(8,128)S(1)}, u32[]{:S(2)}, u32[]{:S(2)}) collective-permute-start(f32[130,1,128]{2,0,1:T(8,128)S(1)} %copy.51), channel_id=1, source_target_pairs={{1,0},{2,1},{3,2},{4,3},{5,4},{6,5},{7,6},{8,7},{9,8},{10,9},{11,1... | collective-permute-start | bytes 199688 | tf_op jit(solution)/shard_map/ppermute | solution.py:24
  150.7 5.8 %collective-permute-start.13 = (f32[1,16,128]{2,1,0:T(8,128)S(1)}, f32[1,16,128]{2,1,0:T(8,128)S(1)}, u32[]{:S(2)}, u32[]{:S(2)}) collective-permute-start(f32[1,16,128]{2,1,0:T(8,128)S(1)} %get-tuple-element.417), channel_id=1, source_target_pairs={{0,16},{16,32},{32,48},{48,64},{64,80},{80,96},{96,112},{112,0},{1... | collective-permute-start | bytes 24584 | tf_op jit(solution)/shard_map/ppermute | solution.py:22
  150.8 5.8 %collective-permute-start.14 = (f32[1,16,128]{2,1,0:T(8,128)S(1)}, f32[1,16,128]{2,1,0:T(8,128)S(1)}, u32[]{:S(2)}, u32[]{:S(2)}) collective-permute-start(f32[1,16,128]{2,1,0:T(8,128)S(1)} %get-tuple-element.418), channel_id=1, source_target_pairs={{16,0},{32,16},{48,32},{64,48},{80,64},{96,80},{112,96},{0,112},{1... | collective-permute-start | bytes 24584 | tf_op jit(solution)/shard_map/ppermute | solution.py:24
  156.6 7.9 %collective-permute-start.15 = (f32[130,1,128]{2,0,1:T(8,128)S(1)}, f32[130,1,128]{2,0,1:T(8,128)S(1)}, u32[]{:S(2)}, u32[]{:S(2)}) collective-permute-start(f32[130,1,128]{2,0,1:T(8,128)S(1)} %copy.54), channel_id=1, source_target_pairs={{0,1},{1,2},{2,3},{3,4},{4,5},{5,6},{6,7},{7,8},{8,9},{9,10},{10,1... | collective-permute-start | bytes 199688 | tf_op jit(solution)/shard_map/ppermute | solution.py:22
  157.0 7.6 %collective-permute-start.16 = (f32[130,1,128]{2,0,1:T(8,128)S(1)}, f32[130,1,128]{2,0,1:T(8,128)S(1)}, u32[]{:S(2)}, u32[]{:S(2)}) collective-permute-start(f32[130,1,128]{2,0,1:T(8,128)S(1)} %copy.55), channel_id=1, source_target_pairs={{1,0},{2,1},{3,2},{4,3},{5,4},{6,5},{7,6},{8,7},{9,8},{10,9},{11,1... | collective-permute-start | bytes 199688 | tf_op jit(solution)/shard_map/ppermute | solution.py:24
  166.7 7.2 %copy-start.10 = (s32[256]{0:T(256)S(1)}, s32[256]{0:T(256)}, u32[]{:S(2)}) copy-start(s32[256]{0:T(256)} %param.33) | copy-start | bytes 3076
  169.6 34.0 %copy-start = (f32[128,16,128]{2,1,0:T(8,128)}, f32[128,16,128]{2,1,0:T(8,128)S(1)}, u32[]{:S(2)}) copy-start(f32[128,16,128]{2,1,0:T(8,128)S(1)} %fusion.63) | copy-start | bytes 3145732
  169.6 25.3 %collective-permute-start.17 = (f32[128,16,128]{2,1,0:T(8,128)S(1)}, f32[128,16,128]{2,1,0:T(8,128)S(1)}, u32[]{:S(2)}, u32[]{:S(2)}) collective-permute-start(f32[128,16,128]{2,1,0:T(8,128)S(1)} %fusion.63), channel_id=1, source_target_pairs={{16,0},{32,16},{48,32},{64,48},{80,64},{96,80},{112,96},{0,112},{1... | collective-permute-start | bytes 3145736 | tf_op jit(solution)/shard_map/ppermute | solution.py:12
  194.9 1.0 copy-start.3
  203.6 43.9 %copy-start.8 = (s32[8192]{0:T(1024)S(1)}, s32[8192]{0:T(1024)}, u32[]{:S(2)}) copy-start(s32[8192]{0:T(1024)} %param.30) | copy-start | bytes 98308
  203.6 43.9 %copy-start.9 = (s32[8192]{0:T(1024)S(1)}, s32[8192]{0:T(1024)}, u32[]{:S(2)}) copy-start(s32[8192]{0:T(1024)} %param.29) | copy-start | bytes 98308
  203.6 51.4 %copy-start.4 = (f32[3,4096]{1,0:T(4,128)S(1)}, f32[3,4096]{1,0:T(4,128)}, u32[]{:S(2)}) copy-start(f32[3,4096]{1,0:T(4,128)} %param.27) | copy-start | bytes 147460
  244.0 11.0 %all-to-all-start.2 = ((f32[16,1,256]{2,1,0:T(1,128)}), f32[16,1,256]{2,1,0:T(1,128)S(1)}, u32[]{:S(2)}, u32[]{:S(2)}) async-start(f32[16,1,256]{2,1,0:T(1,128)} %bitcast.16), calls=%async_computation.2 | async-start | bytes 32768 | tf_op jit(solution)/shard_map/all_to_all | solution.py:199
  255.5 16.2 %collective-permute-start.18 = (f32[4,256]{1,0:T(4,128)S(1)}, f32[4,256]{1,0:T(4,128)S(1)}, u32[]{:S(2)}, u32[]{:S(2)}) collective-permute-start(f32[4,256]{1,0:T(4,128)S(1)} %bitcast.138), channel_id=1, source_target_pairs={{0,16},{16,32},{32,48},{48,64},{64,80},{80,96},{96,112},{112,0},{1... | collective-permute-start | bytes 12296 | tf_op jit(solution)/shard_map/ppermute | solution.py:22
  255.6 16.1 %collective-permute-start.19 = (f32[4,256]{1,0:T(4,128)S(1)}, f32[4,256]{1,0:T(4,128)S(1)}, u32[]{:S(2)}, u32[]{:S(2)}) collective-permute-start(f32[4,256]{1,0:T(4,128)S(1)} %bitcast.139), channel_id=1, source_target_pairs={{16,0},{32,16},{48,32},{64,48},{80,64},{96,80},{112,96},{0,112},{1... | collective-permute-start | bytes 12296 | tf_op jit(solution)/shard_map/ppermute | solution.py:24
  271.9 11.5 %copy-start.6 = (f32[8192]{0:T(1024)S(1)}, f32[8192]{0:T(1024)}, u32[]{:S(2)}) copy-start(f32[8192]{0:T(1024)} %param.31) | copy-start | bytes 98308
  271.9 11.5 %copy-start.7 = (s32[8192]{0:T(1024)S(1)}, s32[8192]{0:T(1024)}, u32[]{:S(2)}) copy-start(s32[8192]{0:T(1024)} %param.32) | copy-start | bytes 98308
  283.5 11.5 %copy-start.5 = (f32[3,4096]{1,0:T(4,128)S(1)}, f32[3,4096]{1,0:T(4,128)}, u32[]{:S(2)}) copy-start(f32[3,4096]{1,0:T(4,128)} %param.28) | copy-start | bytes 147460
where the time goes:
time: 300 us; the launch traced here: 296 us
  matrix products  126 us (42%)
  waiting for transfers between devices  66.3 us (22%)
  starting transfers between devices  62.8 us (21%)
  other arithmetic  28.3 us (9%)
  local copies, waits for them, and re-layouts  9.24 us (3%)
    dot_general x12, matrix products, add_block(): lax.dot_general(row_hot, spread, (((0,), (0,)), ((), ())), precision=lax....  67.2 us
    dot_general x21, matrix products, pick_block(): jnp.dot(row_hot, stacked_rows, precision=lax.Precision.HIGHEST, preferred...  58.7 us
    ppermute x9, starting transfers between devices, with_halo(): lax.ppermute(head, axis, [((i + 1) % count, i) for i in range(count)])  39.8 us
    ppermute x2, waiting for transfers between devices, shifted(): return lax.ppermute(block, axis, route)  38.8 us
    ppermute x9, waiting for transfers between devices, with_halo(): lax.ppermute(tail, axis, [(i, (i + 1) % count) for i in range(count)])  12.4 us
    add x3, other arithmetic, advance(): return center + (change + thermal_input)  8.69 us
    concatenate x1, other arithmetic, per_device(): whole = jnp.concatenate([temp_flat, ahead.reshape(1, -1)], axis=1)  7.65 us
    all_to_all x1, waiting for transfers between devices, per_device(): lax.all_to_all(looked.reshape(groups, capacity), 'cross', split_axis=0, c...  7.44 us
  transfers between devices with their start and end apart: 23, of which 10 were waited for; matrix products, arithmetic and copies ran while one was open for 26% of the time, Pallas kernels for 0%

commit v1 on v0

v1 whole, which is shorter than its diff:
```python
import functools

import jax
import jax.numpy as jnp
from jax import lax
from jax.experimental import pallas as pl
from jax.experimental.pallas import tpu as pltpu
from jax.sharding import PartitionSpec as P

f32 = jnp.float32
bf16 = jnp.bfloat16
i32 = jnp.int32
MESH = pl.DeviceIdType.MESH
NT = (((1,), (1,)), ((), ()))
LANES = 128
VMEM = pl.BlockSpec(memory_space=pltpu.VMEM)


def stack(tile, count):
    return jnp.concatenate([tile] * count, axis=0)


def rows16(row):
    return jnp.broadcast_to(row, (16, row.shape[1])).astype(bf16)


def hot(row, iota):
    r = stack(rows16(row), iota.shape[0] // 16)
    return jnp.where(iota == r, jnp.ones_like(iota), jnp.zeros_like(iota))


def spread(row, val, iota):
    r = stack(rows16(row), iota.shape[0] // 16)
    v = stack(rows16(val), iota.shape[0] // 16)
    return jnp.where(iota == r, v, jnp.zeros_like(iota))


def iota_rows(count):
    return lax.broadcasted_iota(i32, (count, LANES), 0).astype(f32).astype(bf16)


def high(v):
    return v.astype(bf16).astype(f32)


def conduct(t):
    return 0.5 + 1.0 / (1.0 + t * t)


def peers(cuts, crosses):
    c, s = lax.axis_index("cut"), lax.axis_index("cross")
    below, above = lax.rem(c + cuts - 1, cuts), lax.rem(c + 1, cuts)
    return c, s, below, above


def greet(cuts, crosses):
    c, s, below, above = peers(cuts, crosses)
    barrier = pltpu.get_barrier_semaphore()

    def one(k, carry):
        pl.semaphore_signal(barrier, inc=1, device_id=(below, k), device_id_type=MESH)
        pl.semaphore_signal(barrier, inc=1, device_id=(above, k), device_id_type=MESH)
        return carry

    lax.fori_loop(0, crosses, one, 0)

    def other(k, carry):
        j = lax.rem(s + k, crosses)
        pl.semaphore_signal(barrier, inc=1, device_id=(c, j), device_id_type=MESH)
        return carry

    lax.fori_loop(1, crosses, other, 0)


def await_all(crosses):
    pl.semaphore_wait(pltpu.get_barrier_semaphore(), 3 * crosses - 1)


def remote(src, dst, send, recv, device):
    return pltpu.make_async_remote_copy(
        src_ref=src, dst_ref=dst, send_sem=send, recv_sem=recv, device_id=device, device_id_type=MESH
    )


def load_table(tab_ref, row_ref, channels, rows, pitch, dest):
    for ch in range(channels):
        for r in range(rows):
            dest[ch * pitch + r : ch * pitch + r + 1, :] = row_ref[ch : ch + 1, r * LANES : (r + 1) * LANES]
    v = dest[...]
    hi = v.astype(bf16)
    n = channels * pitch
    tab_ref[0:n, :] = hi
    tab_ref[n : 2 * n, :] = (v - hi.astype(f32)).astype(bf16)


def pick_small(tab, channels, pitch, high_row, low_row, iota128):
    got = jnp.dot(tab, hot(low_row, iota128), preferred_element_type=f32)
    n = channels * pitch
    s = lax.broadcasted_iota(i32, (pitch, LANES), 0).astype(f32)
    mask = s == high_row
    out = []
    for ch in range(channels):
        v = got[ch * pitch : (ch + 1) * pitch] + got[n + ch * pitch : n + (ch + 1) * pitch]
        out.append(jnp.sum(jnp.where(mask, v, 0.0), axis=0, keepdims=True))
    return out


def exchange_kernel(
    cuts, crosses, loc, gain, mark, temp, kappa, pos, acted, other, exported,
    lists, hx, hy, ghosts, d_own,
    send_lists, ysend, tab, flat, gsend, send_sem, recv_sem, hsend, hrecv,
):
    c, s, below, above = peers(cuts, crosses)
    greet(cuts, crosses)
    w = loc[...].astype(f32)
    flux = mark[...].astype(f32) * gain[...] * 0.5
    per = w.shape[0] // crosses
    for j in range(crosses):
        send_lists[j, 0:per, :] = w[j * per : (j + 1) * per]
        send_lists[j, per : 2 * per, :] = flux[j * per : (j + 1) * per]
    nx = ysend.shape[2]
    ny = temp.shape[0] // nx
    for a, ref in enumerate((temp, kappa)):
        ysend[a, 0] = ref[pl.ds(0, nx, stride=ny), :]
        ysend[a, 1] = ref[pl.ds(ny - 1, nx, stride=ny), :]
    hi_rows = pos.shape[1] // LANES
    load_table(tab, pos, 3, hi_rows, hi_rows, flat)
    iota = iota_rows(LANES)
    table = tab[...]
    gcount = exported.shape[0]
    for r in range(gcount):
        q = exported[r : r + 1, :]
        v = pick_small(table, 3, hi_rows, (q // LANES).astype(f32), (q % LANES).astype(f32), iota)
        for ch in range(3):
            gsend[ch * gcount + r : ch * gcount + r + 1, :] = v[ch]
    await_all(crosses)

    def send_one(k, carry):
        j = lax.rem(s + k, crosses)
        remote(
            send_lists.at[j], lists.at[crosses + s], send_sem.at[crosses + j], recv_sem.at[crosses + s], (above, j)
        ).start()
        return carry

    def send_same(k, carry):
        j = lax.rem(s + k, crosses)
        remote(send_lists.at[j], lists.at[s], send_sem.at[j], recv_sem.at[s], (c, j)).start()
        return carry

    lax.fori_loop(1, crosses, send_same, 0)
    lax.fori_loop(0, crosses, send_one, 0)
    lists[pl.ds(s, 1)] = send_lists[pl.ds(s, 1)]
    left, right = lax.rem(s + crosses - 1, crosses), lax.rem(s + 1, crosses)
    copies = []
    rows = temp.shape[0]
    for a, ref in enumerate((temp, kappa)):
        copies.append(remote(ref.at[pl.ds(rows - ny, ny)], hx.at[a, 0], hsend.at[4 * a], hrecv.at[4 * a], (above, s)))
        copies.append(remote(ref.at[pl.ds(0, ny)], hx.at[a, 1], hsend.at[4 * a + 1], hrecv.at[4 * a + 1], (below, s)))
        copies.append(remote(ysend.at[a, 1], hy.at[a, 0], hsend.at[4 * a + 2], hrecv.at[4 * a + 2], (c, right)))
        copies.append(remote(ysend.at[a, 0], hy.at[a, 1], hsend.at[4 * a + 3], hrecv.at[4 * a + 3], (c, left)))
    copies.append(remote(gsend, ghosts.at[0], hsend.at[8], hrecv.at[8], (above, s)))
    copies.append(remote(gsend, ghosts.at[1], hsend.at[9], hrecv.at[9], (below, s)))
    for copy in copies:
        copy.start()

    def gather(r, carry):
        q = acted[pl.ds(r, 1), :]
        first = pick_small(table, 3, hi_rows, (q // LANES).astype(f32), (q % LANES).astype(f32), iota)
        q = other[pl.ds(r, 1), :]
        second = pick_small(table, 3, hi_rows, (q // LANES).astype(f32), (q % LANES).astype(f32), iota)
        for ch in range(3):
            d_own[ch, pl.ds(r, 1), :] = second[ch] - first[ch]
        return carry

    lax.fori_loop(0, acted.shape[0], gather, 0, unroll=2)

    def take_same(k, carry):
        j = lax.rem(s + k, crosses)
        remote(send_lists.at[j], lists.at[j], send_sem.at[j], recv_sem.at[j], (c, j)).wait()
        return carry

    def take_one(j, carry):
        n = crosses + j
        remote(send_lists.at[j], lists.at[n], send_sem.at[n], recv_sem.at[n], (above, j)).wait()
        return carry

    lax.fori_loop(1, crosses, take_same, 0)
    lax.fori_loop(0, crosses, take_one, 0)
    for copy in copies:
        copy.wait()


def deposit_kernel(crosses, cells, lists, src, row, zed, val, sp, big):
    per = lists.shape[1] // 2
    for b in range(2 * crosses):
        w = lists[b, 0:per, :].astype(i32)
        here = (w >= cells) == (b >= crosses)
        w = w & (cells - 1)
        row[b * per : (b + 1) * per, :] = jnp.where(here, w // LANES, -1).astype(f32)
        zed[b * per : (b + 1) * per, :] = (w % LANES).astype(f32)
        val[b * per : (b + 1) * per, :] = jnp.where(here, lists[b, per : 2 * per, :], 0.0)
    big[...] = iota_rows(256)
    iota = big[...]
    small = iota[:LANES]
    count = row.shape[0]

    def build(r, carry):
        z = zed[pl.ds(r, 1), :]
        v = val[pl.ds(r, 1), :]
        hi = high(v)
        where = pl.ds(pl.multiple_of(r * LANES, LANES), LANES)
        sp[0:LANES, where] = spread(z, hi, small)
        sp[LANES : 2 * LANES, where] = spread(z, v - hi, small)
        return carry

    lax.fori_loop(0, count, build, 0, unroll=2)
    block, depth = 512, 16

    def outer(m, carry):
        first = m.astype(f32) * float(block)

        def inner(k, acc):
            pieces = []
            for h in range(depth):
                r = row[pl.ds(k * depth + h, 1), :] - first
                parts = []
                for g in range(block // 256):
                    q = r - 256.0 * g
                    parts.append(hot(jnp.where((q >= 0) & (q < 256), q, -1.0), iota))
                pieces.append(jnp.concatenate(parts, axis=0))
            where = pl.ds(pl.multiple_of(k * (depth * LANES), depth * LANES), depth * LANES)
            return acc + lax.dot_general(
                jnp.concatenate(pieces, axis=1), sp[:, where], NT, preferred_element_type=f32
            )

        acc = lax.fori_loop(0, count // depth, inner, jnp.zeros((block, 2 * LANES), f32))
        src[pl.ds(pl.multiple_of(m * block, block), block), :] = acc[:, :LANES] + acc[:, LANES:]
        return carry

    lax.fori_loop(0, src.shape[0] // block, outer, 0)


def main_kernel(
    cuts, crosses, temp, kappa, src, row, zed, hx, hy, ghosts, d_own, acted, other, gap, snapped, exported, loc, pos, vel,
    temp_out, pos_out, vel_out,
    ta, tb, ca, cb, ysend, hyt, hcy, tt, big, picked, back, stage, gtemp_send, gtemp, pq, own, tab,
    xs, xr, ys, yr, bs, br, gs, gr,
):
    c, s, below, above = peers(cuts, crosses)
    left, right = lax.rem(s + crosses - 1, crosses), lax.rem(s + 1, crosses)
    greet(cuts, crosses)
    rows = temp.shape[0]
    nx = hy.shape[2]
    ny = rows // nx
    final = crosses - 1
    low_edge, high_edge = s == 0, s == final
    sub = lax.broadcasted_iota(i32, (ny, LANES), 0)
    lane = lax.broadcasted_iota(i32, (ny, LANES), 1)

    def begin(x, carry):
        where = pl.ds(pl.multiple_of(x * ny, ny), ny)
        there = pl.ds(pl.multiple_of(x * ny + ny, ny), ny)
        t = temp[where, :]
        ta[there, :] = t
        ca[there, :] = kappa[where, :] * conduct(t)
        return carry

    lax.fori_loop(0, nx, begin, 0, unroll=4)
    ta[0:ny, :] = hx[0, 0]
    ta[rows + ny : rows + 2 * ny, :] = hx[0, 1]

    def edge(ref, tref):
        ref[0:ny, :] = hx[1, 0] * conduct(tref[0:ny, :])
        ref[rows + ny : rows + 2 * ny, :] = hx[1, 1] * conduct(tref[rows + ny : rows + 2 * ny, :])

    def rim(plane):
        lo = jnp.where(low_edge, 0.0, plane[0])
        hi = jnp.where(high_edge, 0.0, plane[1])
        klo = jnp.where(low_edge, 0.0, hy[1, 0])
        khi = jnp.where(high_edge, 0.0, hy[1, 1])
        hyt[0] = lo
        hyt[1] = hi
        hcy[0] = klo * conduct(lo)
        hcy[1] = khi * conduct(hi)

    def step(tin, cin, tout, cout):
        def body(x, carry):
            t0, c0, before = carry
            where = pl.ds(pl.multiple_of(x * ny, ny), ny)
            here = pl.ds(pl.multiple_of(x * ny + ny, ny), ny)
            ahead = pl.ds(pl.multiple_of(x * ny + 2 * ny, ny), ny)
            t1 = tin[ahead, :]
            c1 = cin[ahead, :]
            fx = (c0 + c1) * (t1 - t0)
            at = pl.ds(x, 1)
            thi = jnp.where(sub == ny - 1, hyt[1, at, :], pltpu.roll(t0, ny - 1, 0))
            chi = jnp.where(sub == ny - 1, hcy[1, at, :], pltpu.roll(c0, ny - 1, 0))
            fy = (c0 + chi) * (thi - t0)
            flo = (hcy[0, at, :] + c0[0:1]) * (t0[0:1] - hyt[0, at, :])
            fy0 = jnp.where(sub == 0, flo, pltpu.roll(fy, 1, 0))
            tz = jnp.where(lane == LANES - 1, 0.0, pltpu.roll(t0, LANES - 1, 1))
            cz = jnp.where(lane == LANES - 1, 0.0, pltpu.roll(c0, LANES - 1, 1))
            fz = (c0 + cz) * (tz - t0)
            fz0 = jnp.where(lane == 0, c0 * t0, pltpu.roll(fz, 1, 1))
            change = 0.5 * (((fx - before) + (fy - fy0)) + (fz - fz0))
            tn = t0 + (change + src[where, :])
            if cout is None:
                tout[where, :] = tn
            else:
                tout[here, :] = tn
                cout[here, :] = kappa[where, :] * conduct(tn)
            return t1, c1, fx

        t0 = tin[ny : 2 * ny, :]
        c0 = cin[ny : 2 * ny, :]
        tm = tin[0:ny, :]
        cm = cin[0:ny, :]
        lax.fori_loop(0, nx, body, (t0, c0, (cm + c0) * (t0 - tm)), unroll=4)

    def send_halo(k, tref):
        ysend[k, 0] = tref[pl.ds(ny, nx, stride=ny), :]
        ysend[k, 1] = tref[pl.ds(2 * ny - 1, nx, stride=ny), :]
        copies = [
            remote(ysend.at[k, 1], stage.at[k, 0], ys.at[2 * k], yr.at[2 * k], (c, right)),
            remote(ysend.at[k, 0], stage.at[k, 1], ys.at[2 * k + 1], yr.at[2 * k + 1], (c, left)),
            remote(
                tref.at[pl.ds(rows, ny)], tref.at[pl.ds(0, ny)], xs.at[2 * k], xr.at[2 * k], (above, s)
            ),
            remote(
                tref.at[pl.ds(ny, ny)], tref.at[pl.ds(rows + ny, ny)], xs.at[2 * k + 1], xr.at[2 * k + 1], (below, s)
            ),
        ]
        for copy in copies:
            copy.start()
        return copies

    edge(ca, ta)
    rim(hy[0])
    step(ta, ca, tb, cb)
    await_all(crosses)
    first = send_halo(0, tb)

    iota = iota_rows(LANES)
    hi_rows = pos.shape[1] // LANES
    gcount = exported.shape[0]
    bond_rows = acted.shape[0]
    gl = jnp.concatenate([ghosts[0], ghosts[1]], axis=0)
    pad = jnp.zeros((LANES - 4 * 3 * gcount, LANES), f32)
    glo = jnp.concatenate([high(gl), gl - high(gl), pad], axis=0).astype(bf16)

    def ghost_pick(r, carry):
        q = other[pl.ds(r, 1), :] - hi_rows * LANES
        got = jnp.dot(glo, hot((q & (LANES - 1)).astype(f32), iota), preferred_element_type=f32)
        got = got[0 : 6 * gcount] + got[6 * gcount : 12 * gcount]
        h = q // LANES
        for ch in range(3):
            v = jnp.zeros((1, LANES), f32)
            for side in range(2):
                for g in range(gcount):
                    n = (side * 3 + ch) * gcount + g
                    v = v + jnp.where((q >= 0) & (h == side * gcount + g), got[n : n + 1], 0.0)
            pq[ch, pl.ds(r, 1), :] = d_own[ch, pl.ds(r, 1), :] + v
        return carry

    lax.fori_loop(0, bond_rows, ghost_pick, 0, unroll=2)
    d = [pq[ch] for ch in range(3)]
    dist = jnp.sqrt(d[0] * d[0] + d[1] * d[1] + d[2] * d[2])
    g = gap[...]
    base = (1.0 - snapped[...].astype(f32)) / jnp.maximum(dist, 0.3)
    p = base * (dist - g)
    q = base * (-0.1 * g)
    for ch in range(3):
        pq[ch] = p * d[ch]
        pq[3 + ch] = q * d[ch]
    iota32 = iota[:hi_rows]

    def scatter(lo, hi):
        n = hi - lo
        depth = 4

        def body(k, acc):
            lhs, rhs = [], []
            for u in range(depth):
                r = k * depth + u
                a = acted[pl.ds(r, 1), :]
                rhs.append(hot((a % LANES).astype(f32), iota))
                h = (a // LANES).astype(f32)
                tops, lows = [], []
                for ch in range(lo, hi):
                    v = pq[ch, pl.ds(r, 1), :]
                    top = high(v)
                    tops.append(spread(h, top, iota32))
                    lows.append(spread(h, v - top, iota32))
                lhs.append(jnp.concatenate(tops + lows, axis=0))
            return acc + lax.dot_general(
                jnp.concatenate(lhs, axis=1), jnp.concatenate(rhs, axis=1), NT, preferred_element_type=f32
            )

        acc = lax.fori_loop(0, bond_rows // depth, body, jnp.zeros((2 * n * hi_rows, LANES), f32))
        return acc[: n * hi_rows] + acc[n * hi_rows :]

    own[...] = scatter(0, 6)

    for copy in first:
        copy.wait()
    edge(cb, tb)
    rim(stage[0])
    step(tb, cb, ta, ca)
    second = send_halo(1, ta)
    big[...] = iota_rows(256)
    for copy in second:
        copy.wait()
    edge(ca, ta)
    rim(stage[1])
    step(ta, ca, temp_out, None)

    for k in range(rows // LANES):
        b = temp_out[k * LANES : (k + 1) * LANES, :].T
        hi = b.astype(bf16)
        tt[0:LANES, k * LANES : (k + 1) * LANES] = hi
        tt[LANES : 2 * LANES, k * LANES : (k + 1) * LANES] = (b - hi.astype(f32)).astype(bf16)
    wide = big[...]
    per = picked.shape[1]
    both = 2
    zs = lax.broadcasted_iota(i32, (LANES, LANES), 0).astype(f32)

    def look(j, slots):
        cols = []
        for n in slots:
            for h in range(per):
                r = row[pl.ds(n * per + h, 1), :]
                parts = []
                for k in range(rows // 256):
                    q = r - 256.0 * k
                    parts.append(hot(jnp.where((q >= 0) & (q < 256), q, -1.0), wide))
                cols.append(jnp.concatenate(parts, axis=0))
        got = jnp.dot(tt[...], jnp.concatenate(cols, axis=1), preferred_element_type=f32)
        got = got[:LANES] + got[LANES:]
        for i, n in enumerate(slots):
            for h in range(per):
                u = i * per + h
                z = zed[pl.ds(n * per + h, 1), :]
                v = jnp.where(zs == z, got[:, u * LANES : (u + 1) * LANES], 0.0)
                picked[n, h : h + 1, :] = jnp.sum(v, axis=0, keepdims=True)

    def look_far(k, carry):
        j = lax.rem(s + k, crosses)
        look(j, (crosses + j, j))
        remote(picked.at[crosses + j], back.at[crosses + s], bs.at[crosses + j], br.at[crosses + s], (below, j)).start()
        remote(picked.at[j], back.at[s], bs.at[j], br.at[s], (c, j)).start()
        return carry

    lax.fori_loop(1, crosses, look_far, 0)
    look(s, (crosses + s, s))
    remote(picked.at[crosses + s], back.at[crosses + s], bs.at[crosses + s], br.at[crosses + s], (below, s)).start()
    back[pl.ds(s, 1)] = picked[pl.ds(s, 1)]

    def take_same(k, carry):
        j = lax.rem(s + k, crosses)
        remote(picked.at[j], back.at[j], bs.at[j], br.at[j], (c, j)).wait()
        return carry

    def take_far(j, carry):
        n = crosses + j
        remote(picked.at[n], back.at[n], bs.at[n], br.at[n], (below, j)).wait()
        return carry

    lax.fori_loop(1, crosses, take_same, 0)
    lax.fori_loop(0, crosses, take_far, 0)
    cells = rows * LANES
    warm = jnp.where(
        loc[...] >= cells,
        jnp.concatenate([back[crosses + j] for j in range(crosses)], axis=0),
        jnp.concatenate([back[j] for j in range(crosses)], axis=0),
    )
    whi = warm.astype(bf16)
    tab[...] = jnp.concatenate([whi, (warm - whi.astype(f32)).astype(bf16)], axis=0)
    table = tab[...]
    for r in range(gcount):
        e = exported[r : r + 1, :]
        v = pick_small(table, 1, hi_rows, (e // LANES).astype(f32), (e % LANES).astype(f32), iota)
        gtemp_send[r : r + 1, :] = v[0]
    copies = [
        remote(gtemp_send, gtemp.at[0], gs.at[0], gr.at[0], (above, s)),
        remote(gtemp_send, gtemp.at[1], gs.at[1], gr.at[1], (below, s)),
    ]
    for copy in copies:
        copy.start()

    def warm_own(r, carry):
        e = other[pl.ds(r, 1), :]
        v = pick_small(table, 1, hi_rows, (e // LANES).astype(f32), (e % LANES).astype(f32), iota)
        pq[0, pl.ds(r, 1), :] = v[0]
        return carry

    lax.fori_loop(0, bond_rows, warm_own, 0, unroll=2)
    for copy in copies:
        copy.wait()
    gt = jnp.concatenate([gtemp[0], gtemp[1]], axis=0)
    gt = jnp.concatenate([high(gt), gt - high(gt), jnp.zeros((16 - 4 * gcount, LANES), f32)], axis=0).astype(bf16)

    def warm_ghost(r, carry):
        e = other[pl.ds(r, 1), :] - hi_rows * LANES
        got = jnp.dot(gt, hot((e & (LANES - 1)).astype(f32), iota), preferred_element_type=f32)
        got = got[0 : 2 * gcount] + got[2 * gcount : 4 * gcount]
        h = e // LANES
        v = pq[0, pl.ds(r, 1), :]
        for n in range(2 * gcount):
            v = v + jnp.where((e >= 0) & (h == n), got[n : n + 1], 0.0)
        for ch in range(3):
            pq[3 + ch, pl.ds(r, 1), :] = pq[3 + ch, pl.ds(r, 1), :] * v
        return carry

    lax.fori_loop(0, bond_rows, warm_ghost, 0, unroll=2)
    extra = scatter(3, 6)
    base = own[...]
    n = 3 * hi_rows
    force = base[:n] + extra + jnp.concatenate([warm] * 3, axis=0) * base[n:]
    for ch in range(3):
        for r in range(hi_rows):
            where = slice(r * LANES, (r + 1) * LANES)
            v = vel[ch : ch + 1, where] + 0.5 * force[ch * hi_rows + r : ch * hi_rows + r + 1]
            vel_out[ch : ch + 1, where] = v
            pos_out[ch : ch + 1, where] = pos[ch : ch + 1, where] + 0.5 * v


def per_device(
    cuts, crosses, temp, kappa, locator, gain, mark, pos, vel, acted, other, gap, snapped, exported
):
    nx, ny, nz = temp.shape
    rows = nx * ny
    temp2, kappa2 = temp.reshape(rows, nz), kappa.reshape(rows, nz)
    flat = lambda a: a.reshape(-1, LANES)
    loc, gain, mark = flat(locator), flat(gain), flat(mark)
    acted, other, gap, snapped, exported = map(flat, (acted, other, gap, snapped, exported))
    hi_rows = loc.shape[0]
    per = hi_rows // crosses
    gcount = exported.shape[0]
    bonds = acted.shape[0]
    shape = jax.ShapeDtypeStruct
    dma = pltpu.SemaphoreType.DMA
    lists, hx, hy, ghosts, d_own = pl.pallas_call(
        functools.partial(exchange_kernel, cuts, crosses),
        out_shape=(
            shape((2 * crosses, 2 * per, LANES), f32),
            shape((2, 2, ny, nz), f32),
            shape((2, 2, nx, nz), f32),
            shape((2, 3 * gcount, LANES), f32),
            shape((3, bonds, LANES), f32),
        ),
        in_specs=[VMEM] * 9,
        out_specs=(VMEM,) * 5,
        scratch_shapes=[
            pltpu.VMEM((crosses, 2 * per, LANES), f32),
            pltpu.VMEM((2, 2, nx, nz), f32),
            pltpu.VMEM((6 * hi_rows, LANES), bf16),
            pltpu.VMEM((3 * hi_rows, LANES), f32),
            pltpu.VMEM((3 * gcount, LANES), f32),
            dma((2 * crosses,)),
            dma((2 * crosses,)),
            dma((10,)),
            dma((10,)),
        ],
        compiler_params=pltpu.CompilerParams(collective_id=0, has_side_effects=True),
        name="exchange",
    )(loc, gain, mark, temp2, kappa2, pos, acted, other, exported)
    lr = 2 * crosses * per
    src, row, zed = pl.pallas_call(
        functools.partial(deposit_kernel, crosses, rows * nz),
        out_shape=(shape((rows, nz), f32), shape((lr, LANES), f32), shape((lr, LANES), f32)),
        in_specs=[VMEM],
        out_specs=(VMEM,) * 3,
        scratch_shapes=[
            pltpu.VMEM((lr, LANES), f32),
            pltpu.VMEM((2 * LANES, lr * LANES), bf16),
            pltpu.VMEM((256, LANES), bf16),
        ],
        name="deposit",
    )(lists)
    temp_new, pos_new, vel_new = pl.pallas_call(
        functools.partial(main_kernel, cuts, crosses),
        out_shape=(shape((rows, nz), f32), shape(pos.shape, f32), shape(vel.shape, f32)),
        in_specs=[VMEM] * 17,
        out_specs=(VMEM,) * 3,
        scratch_shapes=[
            pltpu.VMEM((rows + 2 * ny, nz), f32),
            pltpu.VMEM((rows + 2 * ny, nz), f32),
            pltpu.VMEM((rows + 2 * ny, nz), f32),
            pltpu.VMEM((rows + 2 * ny, nz), f32),
            pltpu.VMEM((2, 2, nx, nz), f32),
            pltpu.VMEM((2, nx, nz), f32),
            pltpu.VMEM((2, nx, nz), f32),
            pltpu.VMEM((2 * nz, rows), bf16),
            pltpu.VMEM((256, LANES), bf16),
            pltpu.VMEM((2 * crosses, per, LANES), f32),
            pltpu.VMEM((2 * crosses, per, LANES), f32),
            pltpu.VMEM((2, 2, nx, nz), f32),
            pltpu.VMEM((gcount, LANES), f32),
            pltpu.VMEM((2, gcount, LANES), f32),
            pltpu.VMEM((6, bonds, LANES), f32),
            pltpu.VMEM((6 * hi_rows, LANES), f32),
            pltpu.VMEM((2 * hi_rows, LANES), bf16),
            dma((4,)),
            dma((4,)),
            dma((4,)),
            dma((4,)),
            dma((2 * crosses,)),
            dma((2 * crosses,)),
            dma((2,)),
            dma((2,)),
        ],
        compiler_params=pltpu.CompilerParams(collective_id=1, has_side_effects=True),
        name="heat_and_bonds",
    )(temp2, kappa2, src, row, zed, hx, hy, ghosts, d_own, acted, other, gap, snapped, exported, loc, pos, vel)
    return temp_new.reshape(nx, ny, nz), pos_new, vel_new


def solution(mesh):
    both = P(("cut", "cross"))
    return jax.shard_map(
        functools.partial(per_device, mesh.shape["cut"], mesh.shape["cross"]),
        mesh=mesh,
        in_specs=(P("cut", "cross", None),) * 2
        + (both,) * 3
        + (P(None, ("cut", "cross")),) * 2
        + (both,) * 5,
        out_specs=(P("cut", "cross", None), P(None, ("cut", "cross")), P(None, ("cut", "cross"))),
        check_vma=False,
    )
```

time: 300 us -> 105 us (0.35); the launches traced: 296 us -> 104 us
  matrix products: 126 us -> 0 us
  Pallas kernels: 0 us -> 99.8 us
  waiting for transfers between devices: 66.3 us -> 0 us
  starting transfers between devices: 62.8 us -> 0 us
  other arithmetic: 28.3 us -> 0 us
  local copies, waits for them, and re-layouts: 9.24 us -> 3.79 us
    dot_general x33 -> x0, matrix products: 126 us -> none  [the longest x12 67.2 us: add_block(): lax.dot_general(row_hot, spread, (((0,), (0,)), ((), ())), precision=lax....]
    pallas_call x0 -> x3, Pallas kernels: none -> 99.8 us  [the longest x1 63.7 us: per_device(): pl.pallas_call(functools.partial(main_kernel, cuts, crosses), out_shape=(...]
    ppermute x20 -> x0, waiting for transfers between devices: 52.6 us -> none  [the longest x2 38.8 us: shifted(): return lax.ppermute(block, axis, route)]
    ppermute x20 -> x0, starting transfers between devices: 47.5 us -> none  [the longest x9 39.8 us: with_halo(): lax.ppermute(head, axis, [((i + 1) % count, i) for i in range(count)])]
    all_to_all x3 -> x0, starting transfers between devices: 15.3 us -> none  [the longest x1 6.74 us: per_device(): lax.all_to_all(patch_locator.reshape(groups, capacity), 'cross', split_ax...]
    all_to_all x3 -> x0, waiting for transfers between devices: 13.7 us -> none  [the longest x1 7.44 us: per_device(): lax.all_to_all(looked.reshape(groups, capacity), 'cross', split_axis=0, c...]
    add x5 -> x0, other arithmetic: 9.45 us -> none  [the longest x3 8.69 us: advance(): return center + (change + thermal_input)]
    mul x14 -> x0, other arithmetic: 7.96 us -> none  [the longest x3 5.13 us: advance(): conduct_full = kappa_full * conduct(temp_full)]
  transfers between devices with their start and end apart: 23 -> 0, of which waited for: 10 -> 0; matrix products, arithmetic and copies ran while one was open for 26% -> 0% of each run, Pallas kernels for 0% -> 0%
where the time goes in v1:
time: 105 us; the launch traced here: 104 us
  Pallas kernels  99.8 us (95%)
  local copies, waits for them, and re-layouts  3.79 us (4%)
    pallas_call x1, Pallas kernels, per_device(): pl.pallas_call(functools.partial(main_kernel, cuts, crosses), out_shape=(...  63.7 us
    pallas_call x1, Pallas kernels, per_device(): pl.pallas_call(functools.partial(exchange_kernel, cuts, crosses), out_sha...  19.8 us
    pallas_call x1, Pallas kernels, per_device(): pl.pallas_call(functools.partial(deposit_kernel, crosses, rows * nz), out...  16.2 us
    unnamed x7, local copies, waits for them, and re-layouts  3.79 us

profile of v1, /device:TPU:0, one launch (start us, length us, event | category | flops | bytes accessed | tf_op | source)
XLA Modules:
  0.0 104.2 jit_solution(11480766815290837107)
XLA Ops:
  0.6 19.8 %exchange.1 = (f32[32,4,128]{2,1,0:T(4,128)}, f32[2,2,16,128]{3,2,1,0:T(8,128)}, f32[2,2,128,128]{3,2,1,0:T(8,128)}, f32[2,6,128]{2,1,0:T(8,128)}, f32[3,64,128]{2,1,0:T(8,128)}) custom-call(s32[32,128]{1,0:T(8,128)} %bitcast.20, f32[32,128]{1,0:T(8,128)} %bitcast.24, s32[32,128]{1,0:T(8,128)} %bitcast.25, f32[2048,128]{1,0:T(8,128)} %bitcast.11, ...), custom_call_target="tpu_custom_call" | custom-call | tf_op jit(solution)/shard_map/exchange/pallas_call | solution.py:542
  20.5 16.2 %deposit.1 = (f32[2048,128]{1,0:T(8,128)}, f32[64,128]{1,0:T(8,128)}, f32[64,128]{1,0:T(8,128)}) custom-call(f32[32,4,128]{2,1,0:T(4,128)} %get-tuple-element.14.lists), custom_call_target="tpu_custom_call" | custom-call | tf_op jit(solution)/shard_map/deposit/pallas_call | solution.py:568
  36.7 63.7 %heat_and_bonds.1 = (f32[2048,128]{1,0:T(8,128)}, f32[3,4096]{1,0:T(4,128)}, f32[3,4096]{1,0:T(4,128)}) custom-call(f32[2048,128]{1,0:T(8,128)} %bitcast.12, f32[2048,128]{1,0:T(8,128)} %bitcast.14, f32[2048,128]{1,0:T(8,128)} %get-tuple-element.15.src, f32[64,128]{1,0:T(8,128)} %get-tuple-element.16.row, f32[64,128]{1,0:T(8,128)} %get-tuple-element.17.zed, ...), custom_call_target="tpu_custom_call" | custom-call | tf_op jit(solution)/shard_map/heat_and_bonds/pallas_call | solution.py:580
  100.4 0.0 copy-start.1
  100.4 2.3 %copy.18 = f32[128,16,128]{2,1,0:T(8,128)} copy(f32[128,16,128]{2,1,0:T(8,128)} %bitcast.15) | data formatting | bytes 2097152
  102.7 0.0 copy-done.1
  102.7 0.0 copy-start
  102.7 0.6 copy.19
  103.4 0.2 copy-done
  103.6 0.6 copy.20
Async XLA Ops:
  100.4 2.3 %copy-start.1 = (f32[3,4096]{1,0:T(4,128)S(1)}, f32[3,4096]{1,0:T(4,128)}, u32[]{:S(2)}) copy-start(f32[3,4096]{1,0:T(4,128)} %get-tuple-element.29) | copy-start | bytes 147460
  102.7 0.9 copy-start

commit v2 on v1

v2 whole, which is shorter than its diff:
```python
import functools

import jax
import jax.numpy as jnp
from jax import lax
from jax.experimental import pallas as pl
from jax.experimental.pallas import tpu as pltpu
from jax.sharding import PartitionSpec as P

f32 = jnp.float32
bf16 = jnp.bfloat16
i32 = jnp.int32
MESH = pl.DeviceIdType.MESH
NT = (((1,), (1,)), ((), ()))
LANES = 128
VMEM = pl.BlockSpec(memory_space=pltpu.VMEM)


def stack(tile, count):
    return jnp.concatenate([tile] * count, axis=0)


def rows16(row):
    return jnp.broadcast_to(row, (16, row.shape[1])).astype(bf16)


def hot(row, iota):
    r = stack(rows16(row), iota.shape[0] // 16)
    return jnp.where(iota == r, jnp.ones_like(iota), jnp.zeros_like(iota))


def spread(row, val, iota):
    r = stack(rows16(row), iota.shape[0] // 16)
    v = stack(rows16(val), iota.shape[0] // 16)
    return jnp.where(iota == r, v, jnp.zeros_like(iota))


def iota_rows(count):
    return lax.broadcasted_iota(i32, (count, LANES), 0).astype(f32).astype(bf16)


def high(v):
    return v.astype(bf16).astype(f32)


def conduct(t):
    return 0.5 + 1.0 / (1.0 + t * t)


def peers(cuts, crosses):
    c, s = lax.axis_index("cut"), lax.axis_index("cross")
    below, above = lax.rem(c + cuts - 1, cuts), lax.rem(c + 1, cuts)
    return c, s, below, above


def greet(cuts, crosses):
    c, s, below, above = peers(cuts, crosses)
    barrier = pltpu.get_barrier_semaphore()

    def one(k, carry):
        pl.semaphore_signal(barrier, inc=1, device_id=(below, k), device_id_type=MESH)
        pl.semaphore_signal(barrier, inc=1, device_id=(above, k), device_id_type=MESH)
        return carry

    lax.fori_loop(0, crosses, one, 0)

    def other(k, carry):
        j = lax.rem(s + k, crosses)
        pl.semaphore_signal(barrier, inc=1, device_id=(c, j), device_id_type=MESH)
        return carry

    lax.fori_loop(1, crosses, other, 0)


def await_all(crosses):
    pl.semaphore_wait(pltpu.get_barrier_semaphore(), 3 * crosses - 1)


def remote(src, dst, send, recv, device):
    return pltpu.make_async_remote_copy(
        src_ref=src, dst_ref=dst, send_sem=send, recv_sem=recv, device_id=device, device_id_type=MESH
    )


def lane_pick(row, index):
    return jnp.take_along_axis(row, index, axis=1, mode="promise_in_bounds")


def table_pick(rows, high_index, low_index, start):
    out = start
    for number, row in rows:
        wide = jnp.broadcast_to(row, low_index.shape)
        out = jnp.where(high_index == number, lane_pick(wide, low_index), out)
    return out


def kernel(
    cuts, crosses, loc, gain, mark, temp, kappa, pos, vel, acted, other, gap, snapped, exported,
    temp_out, pos_out, vel_out,
    lists, send_lists, hx, hy, ysend0, ghosts, gsend,
    row, zed, val, sp, ohl, big, d1, src, ta, tb, ca, cb, ysend, flux, tt, picked, back, stage,
    gtemp_send, gtemp, pq, own,
    send_sem, recv_sem, hsend, hrecv, xs, xr, ys, yr, bs, br, gs, gr,
):
    c, s, below, above = peers(cuts, crosses)
    left, right = lax.rem(s + crosses - 1, crosses), lax.rem(s + 1, crosses)
    greet(cuts, crosses)
    rows = temp.shape[0]
    nx = hy.shape[2]
    ny = rows // nx
    cells = rows * LANES
    hi_rows = loc.shape[0]
    per = hi_rows // crosses
    gcount = exported.shape[0]
    bond_rows = acted.shape[0]

    w = loc[...].astype(f32)
    power = mark[...].astype(f32) * gain[...] * 0.5
    for j in range(crosses):
        send_lists[j, 0:per, :] = w[j * per : (j + 1) * per]
        send_lists[j, per : 2 * per, :] = power[j * per : (j + 1) * per]
    for a, ref in enumerate((temp, kappa)):
        ysend0[a, 0] = ref[pl.ds(0, nx, stride=ny), :]
        ysend0[a, 1] = ref[pl.ds(ny - 1, nx, stride=ny), :]
    e8 = jnp.concatenate([exported[...]] * (8 // gcount), axis=0)
    eh, el = e8 // LANES, e8 % LANES
    zero8 = jnp.zeros((8, LANES), f32)

    def row_of(ref, ch, r):
        return ref[ch : ch + 1, pl.ds(pl.multiple_of(r * LANES, LANES), LANES)]

    def export_rows(r, acc):
        return tuple(table_pick([(r, row_of(pos, ch, r))], eh, el, acc[ch]) for ch in range(3))

    acc = lax.fori_loop(0, hi_rows, export_rows, (zero8,) * 3, unroll=8)
    for ch in range(3):
        gsend[ch * gcount : (ch + 1) * gcount, :] = acc[ch][:gcount]

    group = 16

    def differences(k, carry):
        where = pl.ds(pl.multiple_of(k * group, group), group)
        qa, qb = acted[where, :], other[where, :]
        index = [(q[h : h + 8] // LANES, q[h : h + 8] % LANES) for q in (qa, qb) for h in range(0, group, 8)]

        def one(r, acc):
            out = []
            for ch in range(3):
                wide = jnp.broadcast_to(row_of(pos, ch, r), (8, LANES))
                for n, (h, l) in enumerate(index):
                    out.append(jnp.where(h == r, lane_pick(wide, l), acc[ch * len(index) + n]))
            return tuple(out)

        acc = lax.fori_loop(0, hi_rows, one, (zero8,) * (3 * len(index)), unroll=4)
        half = len(index) // 2
        for ch in range(3):
            for n in range(half):
                first, second = acc[ch * len(index) + n], acc[ch * len(index) + half + n]
                pq[ch, pl.ds(pl.multiple_of(k * group + 8 * n, 8), 8), :] = second - first
        return carry

    lax.fori_loop(0, bond_rows // group, differences, 0)
    await_all(crosses)

    def send_one(k, carry):
        j = lax.rem(s + k, crosses)
        n = crosses + j
        remote(send_lists.at[j], lists.at[crosses + s], send_sem.at[n], recv_sem.at[crosses + s], (above, j)).start()
        return carry

    def send_same(k, carry):
        j = lax.rem(s + k, crosses)
        remote(send_lists.at[j], lists.at[s], send_sem.at[j], recv_sem.at[s], (c, j)).start()
        return carry

    lax.fori_loop(1, crosses, send_same, 0)
    lax.fori_loop(0, crosses, send_one, 0)
    lists[pl.ds(s, 1)] = send_lists[pl.ds(s, 1)]
    early = []
    for a, ref in enumerate((temp, kappa)):
        early.append(remote(ysend0.at[a, 1], hy.at[a, 0], hsend.at[4 * a + 2], hrecv.at[4 * a + 2], (c, right)))
        early.append(remote(ysend0.at[a, 0], hy.at[a, 1], hsend.at[4 * a + 3], hrecv.at[4 * a + 3], (c, left)))
        early.append(remote(ref.at[pl.ds(rows - ny, ny)], hx.at[a, 0], hsend.at[4 * a], hrecv.at[4 * a], (above, s)))
        early.append(remote(ref.at[pl.ds(0, ny)], hx.at[a, 1], hsend.at[4 * a + 1], hrecv.at[4 * a + 1], (below, s)))
    early.append(remote(gsend, ghosts.at[0], hsend.at[8], hrecv.at[8], (above, s)))
    early.append(remote(gsend, ghosts.at[1], hsend.at[9], hrecv.at[9], (below, s)))
    for copy in early:
        copy.start()

    block = 16 * ny

    def begin(b, carry):
        where = pl.ds(pl.multiple_of(b * block, block), block)
        there = pl.ds(pl.multiple_of(b * block + ny, ny), block)
        t = temp[where, :]
        ta[there, :] = t
        ca[there, :] = kappa[where, :] * conduct(t)
        return carry

    lax.fori_loop(0, rows // block, begin, 0)
    big[...] = iota_rows(256)
    iota = big[...]
    small = iota[:LANES]

    def lows(k, carry):
        for u in range(4):
            r = k * 4 + u
            a = (acted[pl.ds(r, 1), :] % LANES).astype(f32)
            ohl[:, pl.ds(pl.multiple_of(r * LANES, LANES), LANES)] = hot(a, small)
        return carry

    lax.fori_loop(0, bond_rows // 4, lows, 0)

    def take_same(k, carry):
        j = lax.rem(s + k, crosses)
        remote(send_lists.at[j], lists.at[j], send_sem.at[j], recv_sem.at[j], (c, j)).wait()
        return carry

    def take_one(j, carry):
        n = crosses + j
        remote(send_lists.at[j], lists.at[n], send_sem.at[n], recv_sem.at[n], (above, j)).wait()
        return carry

    lax.fori_loop(1, crosses, take_same, 0)
    lax.fori_loop(0, crosses, take_one, 0)

    for b in range(2 * crosses):
        q = lists[b, 0:per, :].astype(i32)
        here = (q >= cells) == (b >= crosses)
        q = q & (cells - 1)
        row[b * per : (b + 1) * per, :] = jnp.where(here, q // LANES, -1).astype(f32)
        zed[b * per : (b + 1) * per, :] = (q % LANES).astype(f32)
        val[b * per : (b + 1) * per, :] = jnp.where(here, lists[b, per : 2 * per, :], 0.0)
    count = row.shape[0]

    def build(k, carry):
        for u in range(4):
            r = k * 4 + u
            z = zed[pl.ds(r, 1), :]
            v = val[pl.ds(r, 1), :]
            hi = high(v)
            where = pl.ds(pl.multiple_of(r * LANES, LANES), LANES)
            sp[0:LANES, where] = spread(z, hi, small)
            sp[LANES : 2 * LANES, where] = spread(z, v - hi, small)
        return carry

    lax.fori_loop(0, count // 4, build, 0)
    r_all = row[...].astype(i32)
    y = r_all & (ny - 1)
    y = jnp.where(y == 0, 0, jnp.where(y == ny - 1, 1, y + 1))
    val[...] = jnp.where(r_all < 0, -1, y * nx + r_all // ny).astype(f32)
    tall, depth = 512, 16

    def deposit(m):
        first = m * float(tall)

        def inner(k, acc):
            pieces = []
            for h in range(depth):
                r = val[pl.ds(k * depth + h, 1), :] - first
                parts = []
                for g in range(tall // 256):
                    q = r - 256.0 * g
                    parts.append(hot(jnp.where((q >= 0) & (q < 256), q, -1.0), iota))
                pieces.append(jnp.concatenate(parts, axis=0))
            where = pl.ds(pl.multiple_of(k * (depth * LANES), depth * LANES), depth * LANES)
            return acc + lax.dot_general(
                jnp.concatenate(pieces, axis=1), sp[:, where], NT, preferred_element_type=f32
            )

        acc = lax.fori_loop(0, count // depth, inner, jnp.zeros((tall, 2 * LANES), f32))
        return acc[:, :LANES] + acc[:, LANES:]

    planes = tall // nx
    got = deposit(0.0)
    for n, y in enumerate((0, ny - 1) + tuple(range(1, planes - 1))):
        src[pl.ds(y, nx, stride=ny), :] = got[n * nx : (n + 1) * nx]

    for copy in early:
        copy.wait()

    final = crosses - 1
    low_edge, high_edge = s == 0, s == final
    sub = lax.broadcasted_iota(i32, (ny, LANES), 0)
    lane = lax.broadcasted_iota(i32, (ny, LANES), 1)

    def edge(cref, tref):
        cref[0:ny, :] = hx[1, 0] * conduct(tref[0:ny, :])
        cref[rows + ny : rows + 2 * ny, :] = hx[1, 1] * conduct(tref[rows + ny : rows + 2 * ny, :])

    def rim(tlo, thi, tref, cref):
        for n, (off, plane, k, at) in enumerate(((low_edge, tlo, hy[1, 0], ny), (high_edge, thi, hy[1, 1], 2 * ny - 1))):
            t = jnp.where(off, 0.0, plane)
            cc = jnp.where(off, 0.0, k) * conduct(t)
            t0 = tref[pl.ds(at, nx, stride=ny), :]
            c0 = cref[pl.ds(at, nx, stride=ny), :]
            flux[n] = (cc + c0) * ((t0 - t) if n == 0 else (t - t0))

    def step(tin, cin, emit):
        many = 16

        def body(b, before):
            for u in range(many):
                x = b * many + u
                here = pl.ds(pl.multiple_of(x * ny + ny, ny), ny)
                ahead = pl.ds(pl.multiple_of(x * ny + 2 * ny, ny), ny)
                t0, c0 = tin[here, :], cin[here, :]
                t1, c1 = tin[ahead, :], cin[ahead, :]
                fx = (c0 + c1) * (t1 - t0)
                at = pl.ds(x, 1)
                ahead_t, ahead_c = pltpu.roll(t0, ny - 1, 0), pltpu.roll(c0, ny - 1, 0)
                fy = jnp.where(sub == ny - 1, flux[1, at, :], (c0 + ahead_c) * (ahead_t - t0))
                fy0 = jnp.where(sub == 0, flux[0, at, :], pltpu.roll(fy, 1, 0))
                ct = c0 * t0
                tz, cz = pltpu.roll(t0, LANES - 1, 1), pltpu.roll(c0, LANES - 1, 1)
                fz = jnp.where(lane == LANES - 1, -ct, (c0 + cz) * (tz - t0))
                fz0 = jnp.where(lane == 0, ct, pltpu.roll(fz, 1, 1))
                emit(x, t0 + 0.5 * (((fx - before) + (fy - fy0)) + (fz - fz0)))
                before = fx
            return before

        t0, c0 = tin[ny : 2 * ny, :], cin[ny : 2 * ny, :]
        tm, cm = tin[0:ny, :], cin[0:ny, :]
        lax.fori_loop(0, nx // many, body, (cm + c0) * (t0 - tm))

    def send_x(k, tref):
        copies = [
            remote(tref.at[pl.ds(rows, ny)], tref.at[pl.ds(0, ny)], xs.at[2 * k], xr.at[2 * k], (above, s)),
            remote(
                tref.at[pl.ds(ny, ny)], tref.at[pl.ds(rows + ny, ny)], xs.at[2 * k + 1], xr.at[2 * k + 1], (below, s)
            ),
        ]
        for copy in copies:
            copy.start()
        return copies

    def send_y(k):
        copies = [
            remote(ysend.at[k, 1], stage.at[k, 0], ys.at[2 * k], yr.at[2 * k], (c, right)),
            remote(ysend.at[k, 0], stage.at[k, 1], ys.at[2 * k + 1], yr.at[2 * k + 1], (c, left)),
        ]
        for copy in copies:
            copy.start()
        return copies

    ta[0:ny, :] = hx[0, 0]
    ta[rows + ny : rows + 2 * ny, :] = hx[0, 1]
    edge(ca, ta)
    rim(hy[0, 0], hy[0, 1], ta, ca)

    def emit_first(x, t):
        d1[pl.ds(pl.multiple_of(x * ny, ny), ny), :] = t

    step(ta, ca, emit_first)
    for n, y in enumerate((0, ny - 1)):
        ysend[0, n] = d1[pl.ds(y, nx, stride=ny), :] + src[pl.ds(y, nx, stride=ny), :]
    first = send_y(0)

    def others(m, carry):
        got = deposit(m.astype(f32))
        for n in range(planes):
            src[pl.ds(m * planes + (n - 1), nx, stride=ny), :] = got[n * nx : (n + 1) * nx]
        return carry

    lax.fori_loop(1, rows // tall, others, 0)

    def finish(b, carry):
        where = pl.ds(pl.multiple_of(b * block, block), block)
        there = pl.ds(pl.multiple_of(b * block + ny, ny), block)
        t = d1[where, :] + src[where, :]
        tb[there, :] = t
        cb[there, :] = kappa[where, :] * conduct(t)
        return carry

    lax.fori_loop(0, rows // block, finish, 0)
    first += send_x(0, tb)

    extra_rows = [(hi_rows + side * gcount + g, side, g) for side in range(2) for g in range(gcount)]
    for k in range(0, bond_rows, 8):
        q = other[k : k + 8, :]
        h, l = q // LANES, q % LANES
        for ch in range(3):
            d = pq[ch, k : k + 8, :]
            g = table_pick([(n, ghosts[side, ch * gcount + i : ch * gcount + i + 1, :]) for n, side, i in extra_rows], h, l, zero8)
            pq[ch, k : k + 8, :] = d + g
    d = [pq[ch] for ch in range(3)]
    dist = jnp.sqrt(d[0] * d[0] + d[1] * d[1] + d[2] * d[2])
    g = gap[...]
    base = (1.0 - snapped[...].astype(f32)) / jnp.maximum(dist, 0.3)
    p = base * (dist - g)
    q = base * (-0.1 * g)
    for ch in range(3):
        pq[ch] = p * d[ch]
        pq[3 + ch] = q * d[ch]
    iota32 = iota[:hi_rows]

    def scatter(values):
        def body(k, acc):
            lhs = []
            for u in range(depth):
                r = k * depth + u
                h = (acted[pl.ds(r, 1), :] // LANES).astype(f32)
                tops, bottoms = [], []
                for v in values(r):
                    top = high(v)
                    tops.append(spread(h, top, iota32))
                    bottoms.append(spread(h, v - top, iota32))
                lhs.append(jnp.concatenate(tops + bottoms, axis=0))
            where = pl.ds(pl.multiple_of(k * (depth * LANES), depth * LANES), depth * LANES)
            return acc + lax.dot_general(
                jnp.concatenate(lhs, axis=1), ohl[:, where], NT, preferred_element_type=f32
            )

        n = 3 * hi_rows
        acc = lax.fori_loop(0, bond_rows // depth, body, jnp.zeros((2 * n, LANES), f32))
        return acc[:n] + acc[n:]

    def rows_of(lo):
        return lambda r: [pq[lo + ch, pl.ds(r, 1), :] for ch in range(3)]

    own[0] = scatter(rows_of(0))

    for copy in first:
        copy.wait()
    edge(cb, tb)
    rim(stage[0, 0], stage[0, 1], tb, cb)

    def emit_second(x, t):
        where = pl.ds(pl.multiple_of(x * ny, ny), ny)
        here = pl.ds(pl.multiple_of(x * ny + ny, ny), ny)
        t = t + src[where, :]
        ta[here, :] = t
        ca[here, :] = kappa[where, :] * conduct(t)

    step(tb, cb, emit_second)
    for n, y in enumerate((ny, 2 * ny - 1)):
        ysend[1, n] = ta[pl.ds(y, nx, stride=ny), :]
    second = send_y(1) + send_x(1, ta)
    own[1] = scatter(rows_of(3))
    for copy in second:
        copy.wait()
    edge(ca, ta)
    rim(stage[1, 0], stage[1, 1], ta, ca)

    def emit_third(x, t):
        where = pl.ds(pl.multiple_of(x * ny, ny), ny)
        temp_out[where, :] = t + src[where, :]

    step(ta, ca, emit_third)

    for k in range(rows // LANES):
        b = temp_out[k * LANES : (k + 1) * LANES, :].T
        hi = b.astype(bf16)
        tt[0:LANES, k * LANES : (k + 1) * LANES] = hi
        tt[LANES : 2 * LANES, k * LANES : (k + 1) * LANES] = (b - hi.astype(f32)).astype(bf16)
    zs = lax.broadcasted_iota(i32, (LANES, LANES), 0).astype(f32)

    def look(slots):
        cols = []
        for n in slots:
            for h in range(per):
                r = row[pl.ds(n * per + h, 1), :]
                parts = []
                for k in range(rows // 256):
                    q = r - 256.0 * k
                    parts.append(hot(jnp.where((q >= 0) & (q < 256), q, -1.0), iota))
                cols.append(jnp.concatenate(parts, axis=0))
        got = jnp.dot(tt[...], jnp.concatenate(cols, axis=1), preferred_element_type=f32)
        got = got[:LANES] + got[LANES:]
        for i, n in enumerate(slots):
            for h in range(per):
                u = i * per + h
                z = zed[pl.ds(n * per + h, 1), :]
                v = jnp.where(zs == z, got[:, u * LANES : (u + 1) * LANES], 0.0)
                picked[n, h : h + 1, :] = jnp.sum(v, axis=0, keepdims=True)

    def look_far(k, carry):
        j = lax.rem(s + k, crosses)
        look((crosses + j, j))
        remote(picked.at[crosses + j], back.at[crosses + s], bs.at[crosses + j], br.at[crosses + s], (below, j)).start()
        remote(picked.at[j], back.at[s], bs.at[j], br.at[s], (c, j)).start()
        return carry

    lax.fori_loop(1, crosses, look_far, 0)
    look((crosses + s, s))
    remote(picked.at[crosses + s], back.at[crosses + s], bs.at[crosses + s], br.at[crosses + s], (below, s)).start()
    back[pl.ds(s, 1)] = picked[pl.ds(s, 1)]

    def back_same(k, carry):
        j = lax.rem(s + k, crosses)
        remote(picked.at[j], back.at[j], bs.at[j], br.at[j], (c, j)).wait()
        return carry

    def back_far(j, carry):
        n = crosses + j
        remote(picked.at[n], back.at[n], bs.at[n], br.at[n], (below, j)).wait()
        return carry

    lax.fori_loop(1, crosses, back_same, 0)
    lax.fori_loop(0, crosses, back_far, 0)
    warm = jnp.where(
        loc[...] >= cells,
        jnp.concatenate([back[crosses + j] for j in range(crosses)], axis=0),
        jnp.concatenate([back[j] for j in range(crosses)], axis=0),
    )
    table = [(r, warm[r : r + 1]) for r in range(hi_rows)]
    gtemp_send[...] = table_pick(table, eh, el, zero8)[:gcount]
    copies = [
        remote(gtemp_send, gtemp.at[0], gs.at[0], gr.at[0], (above, s)),
        remote(gtemp_send, gtemp.at[1], gs.at[1], gr.at[1], (below, s)),
    ]
    for copy in copies:
        copy.start()
    partner = []
    for k in range(0, bond_rows, 8):
        q = other[k : k + 8, :]
        partner.append(table_pick(table, q // LANES, q % LANES, zero8))
    for copy in copies:
        copy.wait()
    for n, k in enumerate(range(0, bond_rows, 8)):
        q = other[k : k + 8, :]
        t = table_pick(
            [(m, gtemp[side, i : i + 1, :]) for m, side, i in extra_rows], q // LANES, q % LANES, partner[n]
        )
        for ch in range(3):
            pq[3 + ch, k : k + 8, :] = pq[3 + ch, k : k + 8, :] * t
    force = own[0] + scatter(rows_of(3)) + jnp.concatenate([warm] * 3, axis=0) * own[1]
    for ch in range(3):
        for r in range(hi_rows):
            where = slice(r * LANES, (r + 1) * LANES)
            v = vel[ch : ch + 1, where] + 0.5 * force[ch * hi_rows + r : ch * hi_rows + r + 1]
            vel_out[ch : ch + 1, where] = v
            pos_out[ch : ch + 1, where] = pos[ch : ch + 1, where] + 0.5 * v


def per_device(
    cuts, crosses, temp, kappa, locator, gain, mark, pos, vel, acted, other, gap, snapped, exported
):
    nx, ny, nz = temp.shape
    rows = nx * ny
    flat = lambda a: a.reshape(-1, LANES)
    loc, gain, mark = flat(locator), flat(gain), flat(mark)
    acted, other, gap, snapped, exported = map(flat, (acted, other, gap, snapped, exported))
    hi_rows = loc.shape[0]
    per = hi_rows // crosses
    gcount = exported.shape[0]
    bonds = acted.shape[0]
    lr = 2 * crosses * per
    shape = jax.ShapeDtypeStruct
    dma = pltpu.SemaphoreType.DMA
    vm = pltpu.VMEM
    plane = (2, 2, nx, nz)
    padded = (rows + 2 * ny, nz)
    temp_new, pos_new, vel_new = pl.pallas_call(
        functools.partial(kernel, cuts, crosses),
        out_shape=(shape((rows, nz), f32), shape(pos.shape, f32), shape(vel.shape, f32)),
        in_specs=[VMEM] * 12,
        out_specs=(VMEM,) * 3,
        scratch_shapes=[
            vm((2 * crosses, 2 * per, LANES), f32),
            vm((crosses, 2 * per, LANES), f32),
            vm((2, 2, ny, nz), f32),
            vm(plane, f32),
            vm(plane, f32),
            vm((2, 3 * gcount, LANES), f32),
            vm((3 * gcount, LANES), f32),
            vm((lr, LANES), f32),
            vm((lr, LANES), f32),
            vm((lr, LANES), f32),
            vm((2 * LANES, lr * LANES), bf16),
            vm((LANES, bonds * LANES), bf16),
            vm((256, LANES), bf16),
            vm((rows, nz), f32),
            vm((rows, nz), f32),
            vm(padded, f32),
            vm(padded, f32),
            vm(padded, f32),
            vm(padded, f32),
            vm(plane, f32),
            vm((2, nx, nz), f32),
            vm((2 * nz, rows), bf16),
            vm((2 * crosses, per, LANES), f32),
            vm((2 * crosses, per, LANES), f32),
            vm(plane, f32),
            vm((gcount, LANES), f32),
            vm((2, gcount, LANES), f32),
            vm((6, bonds, LANES), f32),
            vm((2, 3 * hi_rows, LANES), f32),
            dma((2 * crosses,)),
            dma((2 * crosses,)),
            dma((10,)),
            dma((10,)),
            dma((4,)),
            dma((4,)),
            dma((4,)),
            dma((4,)),
            dma((2 * crosses,)),
            dma((2 * crosses,)),
            dma((2,)),
            dma((2,)),
        ],
        compiler_params=pltpu.CompilerParams(collective_id=0, has_side_effects=True),
        name="substeps",
    )(loc, gain, mark, temp.reshape(rows, nz), kappa.reshape(rows, nz), pos, vel, acted, other, gap, snapped, exported)
    return temp_new.reshape(nx, ny, nz), pos_new, vel_new


def solution(mesh):
    both = P(("cut", "cross"))
    return jax.shard_map(
        functools.partial(per_device, mesh.shape["cut"], mesh.shape["cross"]),
        mesh=mesh,
        in_specs=(P("cut", "cross", None),) * 2
        + (both,) * 3
        + (P(None, ("cut", "cross")),) * 2
        + (both,) * 5,
        out_specs=(P("cut", "cross", None), P(None, ("cut", "cross")), P(None, ("cut", "cross"))),
        check_vma=False,
    )
```

time: 105 us -> 78.4 us (0.75)
  Pallas kernels: 99.8 us -> 73.8 us
    pallas_call x3 -> x1, Pallas kernels: 99.8 us -> 73.8 us  [per_device(): pl.pallas_call(functools.partial(kernel, cuts, crosses), out_shape=(shape...]
where the time goes in v2:
time: 78.4 us; the launch traced here: 78.2 us
  Pallas kernels  73.8 us (94%)
  local copies, waits for them, and re-layouts  3.79 us (5%)
    pallas_call x1, Pallas kernels, per_device(): pl.pallas_call(functools.partial(kernel, cuts, crosses), out_shape=(shape...  73.8 us
    unnamed x7, local copies, waits for them, and re-layouts  3.79 us

profile of v2, /device:TPU:0, one launch (start us, length us, event | category | flops | bytes accessed | tf_op | source)
XLA Modules:
  0.0 78.2 jit_solution(10528667890553889919)
XLA Ops:
  0.6 73.8 %substeps.1 = (f32[2048,128]{1,0:T(8,128)}, f32[3,4096]{1,0:T(4,128)}, f32[3,4096]{1,0:T(4,128)}) custom-call(s32[32,128]{1,0:T(8,128)} %bitcast.18, f32[32,128]{1,0:T(8,128)} %bitcast.19, s32[32,128]{1,0:T(8,128)} %bitcast.20, f32[2048,128]{1,0:T(8,128)} %bitcast.11, f32[2048,128]{1,0:T(8,128)} %bitcast.12, f32[3,4096]{1,0:T(4,128)} %pos.1, f32[3,4096]{1,0:T(4,128)} %vel.1, ...), custom_call_target="tpu_custom_call" | custom-call | tf_op jit(solution)/shard_map/substeps/pallas_call | solution.py:554
  74.4 0.0 copy-start.1
  74.4 2.3 %copy.18 = f32[128,16,128]{2,1,0:T(8,128)} copy(f32[128,16,128]{2,1,0:T(8,128)} %bitcast.13) | data formatting | bytes 2097152
  76.7 0.0 copy-done.1
  76.7 0.0 copy-start
  76.7 0.6 copy.19
  77.4 0.2 copy-done
  77.6 0.6 copy.20
Async XLA Ops:
  74.4 2.3 %copy-start.1 = (f32[3,4096]{1,0:T(4,128)S(1)}, f32[3,4096]{1,0:T(4,128)}, u32[]{:S(2)}) copy-start(f32[3,4096]{1,0:T(4,128)} %get-tuple-element.13) | copy-start | bytes 147460
  76.7 0.9 %copy-start = (f32[3,4096]{1,0:T(4,128)S(1)}, f32[3,4096]{1,0:T(4,128)}, u32[]{:S(2)}) copy-start(f32[3,4096]{1,0:T(4,128)} %get-tuple-element.14) | copy-start | bytes 147460

commit v3 on v2

--- a/solution.py
+++ b/solution.py
@@ -14,6 +14,7 @@
 NT = (((1,), (1,)), ((), ()))
 LANES = 128
 VMEM = pl.BlockSpec(memory_space=pltpu.VMEM)
+ANY = pl.BlockSpec(memory_space=pl.ANY)
 
 
 def stack(tile, count):
@@ -57,12 +58,8 @@
     c, s, below, above = peers(cuts, crosses)
     barrier = pltpu.get_barrier_semaphore()
 
-    def one(k, carry):
-        pl.semaphore_signal(barrier, inc=1, device_id=(below, k), device_id_type=MESH)
-        pl.semaphore_signal(barrier, inc=1, device_id=(above, k), device_id_type=MESH)
-        return carry
-
-    lax.fori_loop(0, crosses, one, 0)
+    for device in ((below, s), (above, s)):
+        pl.semaphore_signal(barrier, inc=1, device_id=device, device_id_type=MESH)
 
     def other(k, carry):
         j = lax.rem(s + k, crosses)
@@ -73,7 +70,7 @@
 
 
 def await_all(crosses):
-    pl.semaphore_wait(pltpu.get_barrier_semaphore(), 3 * crosses - 1)
+    pl.semaphore_wait(pltpu.get_barrier_semaphore(), crosses + 1)
 
 
 def remote(src, dst, send, recv, device):
@@ -95,15 +92,21 @@
 
 
 def kernel(
-    cuts, crosses, loc, gain, mark, temp, kappa, pos, vel, acted, other, gap, snapped, exported,
-    temp_out, pos_out, vel_out,
-    lists, send_lists, hx, hy, ysend0, ghosts, gsend,
-    row, zed, val, sp, ohl, big, d1, src, ta, tb, ca, cb, ysend, flux, tt, picked, back, stage,
+    cuts, crosses, loc, gain, mark, temp_hbm, kappa_hbm, pos, acted, other, gap, snapped, exported,
+    temp_hbm_out, force_out,
+    temp, kappa, temp_out, lists, send_lists, hx, hy, ysend0, ghosts, gsend,
+    row, zed, val, sp, ohl, big, d1, src, ta, tb, ca, cb, ysend, flux, tt, picked, far, ret, back, stage,
     gtemp_send, gtemp, pq, own,
-    send_sem, recv_sem, hsend, hrecv, xs, xr, ys, yr, bs, br, gs, gr,
+    send_sem, recv_sem, hsend, hrecv, xs, xr, ys, yr, bs, br, gs, gr, local,
 ):
     c, s, below, above = peers(cuts, crosses)
     left, right = lax.rem(s + crosses - 1, crosses), lax.rem(s + 1, crosses)
+    loads = [
+        pltpu.make_async_copy(temp_hbm, temp, local.at[0]),
+        pltpu.make_async_copy(kappa_hbm, kappa, local.at[1]),
+    ]
+    for load in loads:
+        load.start()
     greet(cuts, crosses)
     rows = temp.shape[0]
     nx = hy.shape[2]
@@ -119,22 +122,25 @@
     for j in range(crosses):
         send_lists[j, 0:per, :] = w[j * per : (j + 1) * per]
         send_lists[j, per : 2 * per, :] = power[j * per : (j + 1) * per]
+    e8 = jnp.concatenate([exported[...]] * (8 // gcount), axis=0)
+    eh, el = e8 // LANES, e8 % LANES
+    zero8 = jnp.zeros((8, LANES), f32)
+
+    def row_of(ref, ch, r):
+        return ref[ch : ch + 1, pl.ds(pl.multiple_of(r * LANES, LANES), LANES)]
+
+    def export_rows(r, acc):
+        return tuple(table_pick([(r, row_of(pos, ch, r))], eh, el, acc[ch]) for ch in range(3))
+
+    acc = lax.fori_loop(0, hi_rows, export_rows, (zero8,) * 3, unroll=8)
+    for ch in range(3):
+        gsend[ch * gcount : (ch + 1) * gcount, :] = acc[ch][:gcount]
+
+    for load in loads:
+        load.wait()
     for a, ref in enumerate((temp, kappa)):
         ysend0[a, 0] = ref[pl.ds(0, nx, stride=ny), :]
         ysend0[a, 1] = ref[pl.ds(ny - 1, nx, stride=ny), :]
-    e8 = jnp.concatenate([exported[...]] * (8 // gcount), axis=0)
-    eh, el = e8 // LANES, e8 % LANES
-    zero8 = jnp.zeros((8, LANES), f32)
-
-    def row_of(ref, ch, r):
-        return ref[ch : ch + 1, pl.ds(pl.multiple_of(r * LANES, LANES), LANES)]
-
-    def export_rows(r, acc):
-        return tuple(table_pick([(r, row_of(pos, ch, r))], eh, el, acc[ch]) for ch in range(3))
-
-    acc = lax.fori_loop(0, hi_rows, export_rows, (zero8,) * 3, unroll=8)
-    for ch in range(3):
-        gsend[ch * gcount : (ch + 1) * gcount, :] = acc[ch][:gcount]
 
     group = 16
 
@@ -159,14 +165,7 @@
                 pq[ch, pl.ds(pl.multiple_of(k * group + 8 * n, 8), 8), :] = second - first
         return carry
 
-    lax.fori_loop(0, bond_rows // group, differences, 0)
     await_all(crosses)
-
-    def send_one(k, carry):
-        j = lax.rem(s + k, crosses)
-        n = crosses + j
-        remote(send_lists.at[j], lists.at[crosses + s], send_sem.at[n], recv_sem.at[crosses + s], (above, j)).start()
-        return carry
 
     def send_same(k, carry):
         j = lax.rem(s + k, crosses)
@@ -174,7 +173,6 @@
         return carry
 
     lax.fori_loop(1, crosses, send_same, 0)
-    lax.fori_loop(0, crosses, send_one, 0)
     lists[pl.ds(s, 1)] = send_lists[pl.ds(s, 1)]
     early = []
     for a, ref in enumerate((temp, kappa)):
@@ -216,21 +214,12 @@
         remote(send_lists.at[j], lists.at[j], send_sem.at[j], recv_sem.at[j], (c, j)).wait()
         return carry
 
-    def take_one(j, carry):
-        n = crosses + j
-        remote(send_lists.at[j], lists.at[n], send_sem.at[n], recv_sem.at[n], (above, j)).wait()
-        return carry
-
     lax.fori_loop(1, crosses, take_same, 0)
-    lax.fori_loop(0, crosses, take_one, 0)
-
-    for b in range(2 * crosses):
-        q = lists[b, 0:per, :].astype(i32)
-        here = (q >= cells) == (b >= crosses)
-        q = q & (cells - 1)
-        row[b * per : (b + 1) * per, :] = jnp.where(here, q // LANES, -1).astype(f32)
-        zed[b * per : (b + 1) * per, :] = (q % LANES).astype(f32)
-        val[b * per : (b + 1) * per, :] = jnp.where(here, lists[b, per : 2 * per, :], 0.0)
+    relay = remote(
+        lists.at[pl.ds(0, crosses)], lists.at[pl.ds(crosses, crosses)], hsend.at[10], hrecv.at[10], (above, s)
+    )
+    relay.start()
+
     count = row.shape[0]
 
     def build(k, carry):
@@ -244,14 +233,24 @@
             sp[LANES : 2 * LANES, where] = spread(z, v - hi, small)
         return carry
 
-    lax.fori_loop(0, count // 4, build, 0)
-    r_all = row[...].astype(i32)
-    y = r_all & (ny - 1)
-    y = jnp.where(y == 0, 0, jnp.where(y == ny - 1, 1, y + 1))
-    val[...] = jnp.where(r_all < 0, -1, y * nx + r_all // ny).astype(f32)
+    def decode(half):
+        for b in range(half * crosses, (half + 1) * crosses):
+            q = lists[b, 0:per, :].astype(i32)
+            here = (q >= cells) == (half == 1)
+            q = q & (cells - 1)
+            row[b * per : (b + 1) * per, :] = jnp.where(here, q // LANES, -1).astype(f32)
+            zed[b * per : (b + 1) * per, :] = (q % LANES).astype(f32)
+            val[b * per : (b + 1) * per, :] = jnp.where(here, lists[b, per : 2 * per, :], 0.0)
+        lax.fori_loop(half * count // 8, (half + 1) * count // 8, build, 0)
+        where = slice(half * count // 2, (half + 1) * count // 2)
+        r_all = row[where, :].astype(i32)
+        y = r_all & (ny - 1)
+        y = jnp.where(y == 0, 0, jnp.where(y == ny - 1, 1, y + 1))
+        val[where, :] = jnp.where(r_all < 0, -1, y * nx + r_all // ny).astype(f32)
+
     tall, depth = 512, 16
 
-    def deposit(m):
+    def deposit(m, begin, end, acc):
         first = m * float(tall)
 
         def inner(k, acc):
@@ -268,11 +267,17 @@
                 jnp.concatenate(pieces, axis=1), sp[:, where], NT, preferred_element_type=f32
             )
 
-        acc = lax.fori_loop(0, count // depth, inner, jnp.zeros((tall, 2 * LANES), f32))
-        return acc[:, :LANES] + acc[:, LANES:]
+        return lax.fori_loop(begin, end, inner, acc)
 
     planes = tall // nx
-    got = deposit(0.0)
+    nothing = jnp.zeros((tall, 2 * LANES), f32)
+    steps = count // depth
+    decode(0)
+    got = deposit(0.0, 0, steps // 2, nothing)
+    relay.wait()
+    decode(1)
+    got = deposit(0.0, steps // 2, steps, got)
+    got = got[:, :LANES] + got[:, LANES:]
     for n, y in enumerate((0, ny - 1) + tuple(range(1, planes - 1))):
         src[pl.ds(y, nx, stride=ny), :] = got[n * nx : (n + 1) * nx]
 
@@ -357,7 +362,8 @@
     first = send_y(0)
 
     def others(m, carry):
-        got = deposit(m.astype(f32))
+        got = deposit(m.astype(f32), 0, steps, nothing)
+        got = got[:, :LANES] + got[:, LANES:]
         for n in range(planes):
             src[pl.ds(m * planes + (n - 1), nx, stride=ny), :] = got[n * nx : (n + 1) * nx]
         return carry
@@ -375,6 +381,50 @@
     lax.fori_loop(0, rows // block, finish, 0)
     first += send_x(0, tb)
 
+    lax.fori_loop(0, bond_rows // group // 2, differences, 0)
+    iota32 = iota[:hi_rows]
+
+    def scatter(values):
+        def body(k, acc):
+            lhs = []
+            for u in range(depth):
+                r = k * depth + u
+                h = (acted[pl.ds(r, 1), :] // LANES).astype(f32)
+                tops, bottoms = [], []
+                for v in values(r):
+                    top = high(v)
+                    tops.append(spread(h, top, iota32))
+                    bottoms.append(spread(h, v - top, iota32))
+                lhs.append(jnp.concatenate(tops + bottoms, axis=0))
+            where = pl.ds(pl.multiple_of(k * (depth * LANES), depth * LANES), depth * LANES)
+            return acc + lax.dot_general(
+                jnp.concatenate(lhs, axis=1), ohl[:, where], NT, preferred_element_type=f32
+            )
+
+        n = 3 * hi_rows
+        acc = lax.fori_loop(0, bond_rows // depth, body, jnp.zeros((2 * n, LANES), f32))
+        return acc[:n] + acc[n:]
+
+    def rows_of(lo):
+        return lambda r: [pq[lo + ch, pl.ds(r, 1), :] for ch in range(3)]
+
+    for copy in first:
+        copy.wait()
+    edge(cb, tb)
+    rim(stage[0, 0], stage[0, 1], tb, cb)
+
+    def emit_second(x, t):
+        where = pl.ds(pl.multiple_of(x * ny, ny), ny)
+        here = pl.ds(pl.multiple_of(x * ny + ny, ny), ny)
+        t = t + src[where, :]
+        ta[here, :] = t
+        ca[here, :] = kappa[where, :] * conduct(t)
+
+    step(tb, cb, emit_second)
+    for n, y in enumerate((ny, 2 * ny - 1)):
+        ysend[1, n] = ta[pl.ds(y, nx, stride=ny), :]
+    second = send_y(1) + send_x(1, ta)
+    lax.fori_loop(bond_rows // group // 2, bond_rows // group, differences, 0)
     extra_rows = [(hi_rows + side * gcount + g, side, g) for side in range(2) for g in range(gcount)]
     for k in range(0, bond_rows, 8):
         q = other[k : k + 8, :]
@@ -392,51 +442,6 @@
     for ch in range(3):
         pq[ch] = p * d[ch]
         pq[3 + ch] = q * d[ch]
-    iota32 = iota[:hi_rows]
-
-    def scatter(values):
-        def body(k, acc):
-            lhs = []
-            for u in range(depth):
-                r = k * depth + u
-                h = (acted[pl.ds(r, 1), :] // LANES).astype(f32)
-                tops, bottoms = [], []
-                for v in values(r):
-                    top = high(v)
-                    tops.append(spread(h, top, iota32))
-                    bottoms.append(spread(h, v - top, iota32))
-                lhs.append(jnp.concatenate(tops + bottoms, axis=0))
-            where = pl.ds(pl.multiple_of(k * (depth * LANES), depth * LANES), depth * LANES)
-            return acc + lax.dot_general(
-                jnp.concatenate(lhs, axis=1), ohl[:, where], NT, preferred_element_type=f32
-            )
-
-        n = 3 * hi_rows
-        acc = lax.fori_loop(0, bond_rows // depth, body, jnp.zeros((2 * n, LANES), f32))
-        return acc[:n] + acc[n:]
-
-    def rows_of(lo):
-        return lambda r: [pq[lo + ch, pl.ds(r, 1), :] for ch in range(3)]
-
-    own[0] = scatter(rows_of(0))
-
-    for copy in first:
-        copy.wait()
-    edge(cb, tb)
-    rim(stage[0, 0], stage[0, 1], tb, cb)
-
-    def emit_second(x, t):
-        where = pl.ds(pl.multiple_of(x * ny, ny), ny)
-        here = pl.ds(pl.multiple_of(x * ny + ny, ny), ny)
-        t = t + src[where, :]
-        ta[here, :] = t
-        ca[here, :] = kappa[where, :] * conduct(t)
-
-    step(tb, cb, emit_second)
-    for n, y in enumerate((ny, 2 * ny - 1)):
-        ysend[1, n] = ta[pl.ds(y, nx, stride=ny), :]
-    second = send_y(1) + send_x(1, ta)
-    own[1] = scatter(rows_of(3))
     for copy in second:
         copy.wait()
     edge(ca, ta)
@@ -447,6 +452,8 @@
         temp_out[where, :] = t + src[where, :]
 
     step(ta, ca, emit_third)
+    store = pltpu.make_async_copy(temp_out, temp_hbm_out, local.at[2])
+    store.start()
 
     for k in range(rows // LANES):
         b = temp_out[k * LANES : (k + 1) * LANES, :].T
@@ -474,35 +481,62 @@
                 v = jnp.where(zs == z, got[:, u * LANES : (u + 1) * LANES], 0.0)
                 picked[n, h : h + 1, :] = jnp.sum(v, axis=0, keepdims=True)
 
-    def look_far(k, carry):
-        j = lax.rem(s + k, crosses)
-        look((crosses + j, j))
-        remote(picked.at[crosses + j], back.at[crosses + s], bs.at[crosses + j], br.at[crosses + s], (below, j)).start()
-        remote(picked.at[j], back.at[s], bs.at[j], br.at[s], (c, j)).start()
-        return carry
-
-    lax.fori_loop(1, crosses, look_far, 0)
-    look((crosses + s, s))
-    remote(picked.at[crosses + s], back.at[crosses + s], bs.at[crosses + s], br.at[crosses + s], (below, s)).start()
-    back[pl.ds(s, 1)] = picked[pl.ds(s, 1)]
+    def look_below(k, carry):
+        look((crosses + 2 * k, crosses + 2 * k + 1))
+        return carry
+
+    lax.fori_loop(0, crosses // 2, look_below, 0)
+    hand = remote(picked.at[pl.ds(crosses, crosses)], far, hsend.at[11], hrecv.at[11], (below, s))
+    hand.start()
+
+    def pair(k):
+        return lax.rem(s + 2 * k + 1, crosses), lax.rem(s + 2 * k + 2, crosses)
+
+    def merge(j):
+        m = row[pl.ds(j * per, per), :] < 0
+        return jnp.where(m, far[pl.ds(j, 1)].reshape(per, LANES), picked[pl.ds(j, 1)].reshape(per, LANES))
+
+    def back_to(j):
+        ret[pl.ds(j, 1)] = merge(j).reshape(1, per, LANES)
+        remote(ret.at[j], back.at[s], bs.at[j], br.at[s], (c, j)).start()
+
+    held = 3
+
+    def look_first(k, carry):
+        look(pair(k))
+        return carry
+
+    lax.fori_loop(0, held, look_first, 0)
+    hand.wait()
+
+    def send_held(i, carry):
+        back_to(lax.rem(s + i, crosses))
+        return carry
+
+    lax.fori_loop(1, 2 * held + 1, send_held, 0)
+
+    def look_then(k, carry):
+        a, b = pair(k)
+        look((a, b))
+        back_to(a)
+        back_to(b)
+        return carry
+
+    lax.fori_loop(held, crosses // 2 - 1, look_then, 0)
+    a, b = pair(crosses // 2 - 1)
+    look((a, b))
+    back_to(a)
+    back[pl.ds(s, 1)] = merge(s).reshape(1, per, LANES)
+    own[0] = scatter(rows_of(0))
+    own[1] = scatter(rows_of(3))
 
     def back_same(k, carry):
         j = lax.rem(s + k, crosses)
-        remote(picked.at[j], back.at[j], bs.at[j], br.at[j], (c, j)).wait()
-        return carry
-
-    def back_far(j, carry):
-        n = crosses + j
-        remote(picked.at[n], back.at[n], bs.at[n], br.at[n], (below, j)).wait()
+        remote(ret.at[j], back.at[j], bs.at[j], br.at[j], (c, j)).wait()
         return carry
 
     lax.fori_loop(1, crosses, back_same, 0)
-    lax.fori_loop(0, crosses, back_far, 0)
-    warm = jnp.where(
-        loc[...] >= cells,
-        jnp.concatenate([back[crosses + j] for j in range(crosses)], axis=0),
-        jnp.concatenate([back[j] for j in range(crosses)], axis=0),
-    )
+    warm = jnp.concatenate([back[j] for j in range(crosses)], axis=0)
     table = [(r, warm[r : r + 1]) for r in range(hi_rows)]
     gtemp_send[...] = table_pick(table, eh, el, zero8)[:gcount]
     copies = [
@@ -524,13 +558,30 @@
         )
         for ch in range(3):
             pq[3 + ch, k : k + 8, :] = pq[3 + ch, k : k + 8, :] * t
-    force = own[0] + scatter(rows_of(3)) + jnp.concatenate([warm] * 3, axis=0) * own[1]
+    force_out[...] = own[0] + scatter(rows_of(3)) + jnp.concatenate([warm] * 3, axis=0) * own[1]
+    store.wait()
+
+
+def update_kernel(temp, force, pos, vel, temp_out, pos_out, vel_out, held, sems):
+    parts = held.shape[0]
+    rows = held.shape[1]
+    where = [pl.ds(n * rows, rows) for n in range(parts)]
+    loads = [pltpu.make_async_copy(temp.at[w], held.at[n], sems.at[0, n]) for n, w in enumerate(where)]
+    stores = [pltpu.make_async_copy(held.at[n], temp_out.at[w], sems.at[1, n]) for n, w in enumerate(where)]
+    for load in loads:
+        load.start()
+    for load, store in zip(loads, stores):
+        load.wait()
+        store.start()
     for ch in range(3):
+        hi_rows = pos.shape[1] // LANES
         for r in range(hi_rows):
-            where = slice(r * LANES, (r + 1) * LANES)
-            v = vel[ch : ch + 1, where] + 0.5 * force[ch * hi_rows + r : ch * hi_rows + r + 1]
-            vel_out[ch : ch + 1, where] = v
-            pos_out[ch : ch + 1, where] = pos[ch : ch + 1, where] + 0.5 * v
+            at = slice(r * LANES, (r + 1) * LANES)
+            v = vel[ch : ch + 1, at] + 0.5 * force[ch * hi_rows + r : ch * hi_rows + r + 1]
+            vel_out[ch : ch + 1, at] = v
+            pos_out[ch : ch + 1, at] = pos[ch : ch + 1, at] + 0.5 * v
+    for store in stores:
+        store.wait()
 
 
 def per_device(
@@ -551,12 +602,15 @@
     vm = pltpu.VMEM
     plane = (2, 2, nx, nz)
     padded = (rows + 2 * ny, nz)
-    temp_new, pos_new, vel_new = pl.pallas_call(
+    temp_new, force = pl.pallas_call(
         functools.partial(kernel, cuts, crosses),
-        out_shape=(shape((rows, nz), f32), shape(pos.shape, f32), shape(vel.shape, f32)),
-        in_specs=[VMEM] * 12,
-        out_specs=(VMEM,) * 3,
+        out_shape=(shape((rows, nz), f32), shape((3 * hi_rows, LANES), f32)),
+        in_specs=[VMEM] * 3 + [ANY] * 2 + [VMEM] * 6,
+        out_specs=(ANY, VMEM),
         scratch_shapes=[
+            vm((rows, nz), f32),
+            vm((rows, nz), f32),
+            vm((rows, nz), f32),
             vm((2 * crosses, 2 * per, LANES), f32),
             vm((crosses, 2 * per, LANES), f32),
             vm((2, 2, ny, nz), f32),
@@ -580,28 +634,39 @@
             vm((2, nx, nz), f32),
             vm((2 * nz, rows), bf16),
             vm((2 * crosses, per, LANES), f32),
-            vm((2 * crosses, per, LANES), f32),
+            vm((crosses, per, LANES), f32),
+            vm((crosses, per, LANES), f32),
+            vm((crosses, per, LANES), f32),
             vm(plane, f32),
             vm((gcount, LANES), f32),
             vm((2, gcount, LANES), f32),
             vm((6, bonds, LANES), f32),
             vm((2, 3 * hi_rows, LANES), f32),
-            dma((2 * crosses,)),
-            dma((2 * crosses,)),
-            dma((10,)),
-            dma((10,)),
+            dma((crosses,)),
+            dma((crosses,)),
+            dma((12,)),
+            dma((12,)),
             dma((4,)),
             dma((4,)),
             dma((4,)),
             dma((4,)),
-            dma((2 * crosses,)),
-            dma((2 * crosses,)),
+            dma((crosses,)),
+            dma((crosses,)),
             dma((2,)),
             dma((2,)),
+            dma((3,)),
         ],
         compiler_params=pltpu.CompilerParams(collective_id=0, has_side_effects=True),
         name="substeps",
-    )(loc, gain, mark, temp.reshape(rows, nz), kappa.reshape(rows, nz), pos, vel, acted, other, gap, snapped, exported)
+    )(loc, gain, mark, temp.reshape(rows, nz), kappa.reshape(rows, nz), pos, acted, other, gap, snapped, exported)
+    temp_new, pos_new, vel_new = pl.pallas_call(
+        update_kernel,
+        out_shape=(shape((rows, nz), f32), shape(pos.shape, f32), shape(vel.shape, f32)),
+        in_specs=[ANY] + [VMEM] * 3,
+        out_specs=(ANY, VMEM, VMEM),
+        scratch_shapes=[vm((4, rows // 4, nz), f32), dma((2, 4))],
+        name="update",
+    )(temp_new, force, pos, vel)
     return temp_new.reshape(nx, ny, nz), pos_new, vel_new
 
 

time: 78.4 us -> 72.9 us (0.930)
  local copies, waits for them, and re-layouts: 3.79 us -> 0 us
  Pallas kernels: 73.8 us -> 72 us
    pallas_call x1, Pallas kernels: 73.8 us -> 68.5 us  [per_device(): pl.pallas_call(functools.partial(kernel, cuts, crosses), out_shape=(shape...]
    unnamed x7 -> x0, local copies, waits for them, and re-layouts: 3.79 us -> none
    pallas_call x0 -> x1, Pallas kernels: none -> 3.53 us  [per_device(): pl.pallas_call(update_kernel, out_shape=(shape((rows, nz), f32), shape(po...]
where the time goes in v3:
time: 72.9 us; the launch traced here: 72.6 us
  Pallas kernels  72 us (99%)
    pallas_call x1, Pallas kernels, per_device(): pl.pallas_call(functools.partial(kernel, cuts, crosses), out_shape=(shape...  68.5 us
    pallas_call x1, Pallas kernels, per_device(): pl.pallas_call(update_kernel, out_shape=(shape((rows, nz), f32), shape(po...  3.53 us

profile of v3, /device:TPU:0, one launch (start us, length us, event | category | flops | bytes accessed | tf_op | source)
XLA Modules:
  0.0 72.6 jit_solution(357899140135647399)
XLA Ops:
  0.6 68.5 %substeps.1 = (f32[2048,128]{1,0:T(8,128)}, f32[96,128]{1,0:T(8,128)}) custom-call(s32[32,128]{1,0:T(8,128)} %bitcast.17, f32[32,128]{1,0:T(8,128)} %bitcast.18, s32[32,128]{1,0:T(8,128)} %bitcast.19, f32[2048,128]{1,0:T(8,128)} %bitcast.11, f32[2048,128]{1,0:T(8,128)} %bitcast.12, f32[3,4096]{1,0:T(4,128)} %pos.3, s32[64,128]{1,0:T(8,128)} %bitcast.13, ...), custom_call_target="tpu_custom_call" | custom-call | tf_op jit(solution)/shard_map/substeps/pallas_call | solution.py:605
  69.1 3.5 %update.1 = (f32[2048,128]{1,0:T(8,128)}, f32[3,4096]{1,0:T(4,128)}, f32[3,4096]{1,0:T(4,128)}) custom-call(f32[2048,128]{1,0:T(8,128)} %get-tuple-element.8.temp, f32[96,128]{1,0:T(8,128)} %get-tuple-element.9.force, f32[3,4096]{1,0:T(4,128)} %pos.3, f32[3,4096]{1,0:T(4,128)} %vel.1), custom_call_target="tpu_custom_call" | custom-call | tf_op jit(solution)/shard_map/update/pallas_call | solution.py:662

commit v4 on v3

--- a/solution.py
+++ b/solution.py
@@ -92,19 +92,19 @@
 
 
 def kernel(
-    cuts, crosses, loc, gain, mark, temp_hbm, kappa_hbm, pos, acted, other, gap, snapped, exported,
-    temp_hbm_out, force_out,
-    temp, kappa, temp_out, lists, send_lists, hx, hy, ysend0, ghosts, gsend,
+    cuts, crosses, *refs
+):
+    inputs, (temp_hbm_out, force_out) = refs[:11], refs[11:13]
+    loc, gain, mark, exported, pos, temp, kappa, acted, other, gap, snapped = refs[13:24]
+    (
+    temp_out, lists, send_lists, hx, hy, ysend0, ghosts, gsend,
     row, zed, val, sp, ohl, big, d1, src, ta, tb, ca, cb, ysend, flux, tt, picked, far, ret, back, stage,
     gtemp_send, gtemp, pq, own,
-    send_sem, recv_sem, hsend, hrecv, xs, xr, ys, yr, bs, br, gs, gr, local,
-):
+    send_sem, recv_sem, hsend, hrecv, xs, xr, ys, yr, zs_sem, zr_sem, bs, br, gs, gr, local,
+    ) = refs[24:]
     c, s, below, above = peers(cuts, crosses)
     left, right = lax.rem(s + crosses - 1, crosses), lax.rem(s + 1, crosses)
-    loads = [
-        pltpu.make_async_copy(temp_hbm, temp, local.at[0]),
-        pltpu.make_async_copy(kappa_hbm, kappa, local.at[1]),
-    ]
+    loads = [pltpu.make_async_copy(a, b, local.at[n]) for n, (a, b) in enumerate(zip(inputs, refs[13:24]))]
     for load in loads:
         load.start()
     greet(cuts, crosses)
@@ -117,6 +117,8 @@
     gcount = exported.shape[0]
     bond_rows = acted.shape[0]
 
+    for load in loads[:5]:
+        load.wait()
     w = loc[...].astype(f32)
     power = mark[...].astype(f32) * gain[...] * 0.5
     for j in range(crosses):
@@ -136,7 +138,7 @@
     for ch in range(3):
         gsend[ch * gcount : (ch + 1) * gcount, :] = acc[ch][:gcount]
 
-    for load in loads:
+    for load in loads[5:]:
         load.wait()
     for a, ref in enumerate((temp, kappa)):
         ysend0[a, 0] = ref[pl.ds(0, nx, stride=ny), :]
@@ -223,8 +225,8 @@
     count = row.shape[0]
 
     def build(k, carry):
-        for u in range(4):
-            r = k * 4 + u
+        for u in range(8):
+            r = k * 8 + u
             z = zed[pl.ds(r, 1), :]
             v = val[pl.ds(r, 1), :]
             hi = high(v)
@@ -241,7 +243,7 @@
             row[b * per : (b + 1) * per, :] = jnp.where(here, q // LANES, -1).astype(f32)
             zed[b * per : (b + 1) * per, :] = (q % LANES).astype(f32)
             val[b * per : (b + 1) * per, :] = jnp.where(here, lists[b, per : 2 * per, :], 0.0)
-        lax.fori_loop(half * count // 8, (half + 1) * count // 8, build, 0)
+        lax.fori_loop(half * count // 16, (half + 1) * count // 16, build, 0)
         where = slice(half * count // 2, (half + 1) * count // 2)
         r_all = row[where, :].astype(i32)
         y = r_all & (ny - 1)
@@ -301,8 +303,9 @@
             c0 = cref[pl.ds(at, nx, stride=ny), :]
             flux[n] = (cc + c0) * ((t0 - t) if n == 0 else (t - t0))
 
-    def step(tin, cin, emit):
-        many = 16
+    many = 16
+
+    def step(tin, cin, emit, parts=1, done=None):
 
         def body(b, before):
             for u in range(many):
@@ -326,7 +329,17 @@
 
         t0, c0 = tin[ny : 2 * ny, :], cin[ny : 2 * ny, :]
         tm, cm = tin[0:ny, :], cin[0:ny, :]
-        lax.fori_loop(0, nx // many, body, (cm + c0) * (t0 - tm))
+        turns = nx // many // parts
+
+        def piece(k, before):
+            before = lax.fori_loop(k * turns, (k + 1) * turns, body, before)
+            done(k)
+            return before
+
+        if done is None:
+            lax.fori_loop(0, turns, body, (cm + c0) * (t0 - tm))
+        else:
+            lax.fori_loop(0, parts, piece, (cm + c0) * (t0 - tm))
 
     def send_x(k, tref):
         copies = [
@@ -339,10 +352,10 @@
             copy.start()
         return copies
 
-    def send_y(k):
+    def send_y():
         copies = [
-            remote(ysend.at[k, 1], stage.at[k, 0], ys.at[2 * k], yr.at[2 * k], (c, right)),
-            remote(ysend.at[k, 0], stage.at[k, 1], ys.at[2 * k + 1], yr.at[2 * k + 1], (c, left)),
+            remote(ysend.at[0, 1], stage.at[0, 0], ys.at[0], yr.at[0], (c, right)),
+            remote(ysend.at[0, 0], stage.at[0, 1], ys.at[1], yr.at[1], (c, left)),
         ]
         for copy in copies:
             copy.start()
@@ -359,7 +372,7 @@
     step(ta, ca, emit_first)
     for n, y in enumerate((0, ny - 1)):
         ysend[0, n] = d1[pl.ds(y, nx, stride=ny), :] + src[pl.ds(y, nx, stride=ny), :]
-    first = send_y(0)
+    first = send_y()
 
     def others(m, carry):
         got = deposit(m.astype(f32), 0, steps, nothing)
@@ -420,10 +433,25 @@
         ta[here, :] = t
         ca[here, :] = kappa[where, :] * conduct(t)
 
-    step(tb, cb, emit_second)
-    for n, y in enumerate((ny, 2 * ny - 1)):
-        ysend[1, n] = ta[pl.ds(y, nx, stride=ny), :]
-    second = send_y(1) + send_x(1, ta)
+    pieces = 4
+    width = nx // pieces
+
+    def strip(k):
+        at = pl.ds(pl.multiple_of(k * width, width), width)
+        return [
+            remote(ysend.at[1, 1, at], stage.at[1, 0, at], zs_sem.at[k], zr_sem.at[k], (c, right)),
+            remote(ysend.at[1, 0, at], stage.at[1, 1, at], zs_sem.at[pieces + k], zr_sem.at[pieces + k], (c, left)),
+        ]
+
+    def strip_done(k):
+        at = pl.ds(pl.multiple_of(k * width, width), width)
+        for n, y in enumerate((ny, 2 * ny - 1)):
+            ysend[1, n, at, :] = ta[pl.ds(k * (width * ny) + y, width, stride=ny), :]
+        for copy in strip(k):
+            copy.start()
+
+    step(tb, cb, emit_second, pieces, strip_done)
+    second = send_x(1, ta)
     lax.fori_loop(bond_rows // group // 2, bond_rows // group, differences, 0)
     extra_rows = [(hi_rows + side * gcount + g, side, g) for side in range(2) for g in range(gcount)]
     for k in range(0, bond_rows, 8):
@@ -444,6 +472,13 @@
         pq[3 + ch] = q * d[ch]
     for copy in second:
         copy.wait()
+
+    def strip_taken(k, carry):
+        for copy in strip(k):
+            copy.wait()
+        return carry
+
+    lax.fori_loop(0, pieces, strip_taken, 0)
     edge(ca, ta)
     rim(stage[1, 0], stage[1, 1], ta, ca)
 
@@ -452,7 +487,7 @@
         temp_out[where, :] = t + src[where, :]
 
     step(ta, ca, emit_third)
-    store = pltpu.make_async_copy(temp_out, temp_hbm_out, local.at[2])
+    store = pltpu.make_async_copy(temp_out, temp_hbm_out, local.at[11])
     store.start()
 
     for k in range(rows // LANES):
@@ -528,7 +563,6 @@
     back_to(a)
     back[pl.ds(s, 1)] = merge(s).reshape(1, per, LANES)
     own[0] = scatter(rows_of(0))
-    own[1] = scatter(rows_of(3))
 
     def back_same(k, carry):
         j = lax.rem(s + k, crosses)
@@ -549,6 +583,7 @@
     for k in range(0, bond_rows, 8):
         q = other[k : k + 8, :]
         partner.append(table_pick(table, q // LANES, q % LANES, zero8))
+    own[1] = scatter(rows_of(3))
     for copy in copies:
         copy.wait()
     for n, k in enumerate(range(0, bond_rows, 8)):
@@ -562,25 +597,35 @@
     store.wait()
 
 
-def update_kernel(temp, force, pos, vel, temp_out, pos_out, vel_out, held, sems):
+def update_kernel(
+    temp, force_hbm, pos_hbm, vel_hbm, temp_out, pos_out, vel_out, held, force, pos, vel, sems, small
+):
     parts = held.shape[0]
     rows = held.shape[1]
+    first = [
+        pltpu.make_async_copy(a, b, small.at[n])
+        for n, (a, b) in enumerate(((force_hbm, force), (pos_hbm, pos), (vel_hbm, vel)))
+    ]
     where = [pl.ds(n * rows, rows) for n in range(parts)]
     loads = [pltpu.make_async_copy(temp.at[w], held.at[n], sems.at[0, n]) for n, w in enumerate(where)]
     stores = [pltpu.make_async_copy(held.at[n], temp_out.at[w], sems.at[1, n]) for n, w in enumerate(where)]
-    for load in loads:
+    for load in first + loads:
         load.start()
+    for load in first:
+        load.wait()
+    hi_rows = pos.shape[1] // LANES
+    for r in range(hi_rows):
+        at = slice(r * LANES, (r + 1) * LANES)
+        v = vel[:, at] + 0.5 * force[pl.ds(r, 3, stride=hi_rows), :]
+        vel[:, at] = v
+        pos[:, at] = pos[:, at] + 0.5 * v
+    last = [pltpu.make_async_copy(vel, vel_out, small.at[3]), pltpu.make_async_copy(pos, pos_out, small.at[4])]
+    for store in last:
+        store.start()
     for load, store in zip(loads, stores):
         load.wait()
         store.start()
-    for ch in range(3):
-        hi_rows = pos.shape[1] // LANES
-        for r in range(hi_rows):
-            at = slice(r * LANES, (r + 1) * LANES)
-            v = vel[ch : ch + 1, at] + 0.5 * force[ch * hi_rows + r : ch * hi_rows + r + 1]
-            vel_out[ch : ch + 1, at] = v
-            pos_out[ch : ch + 1, at] = pos[ch : ch + 1, at] + 0.5 * v
-    for store in stores:
+    for store in stores + last:
         store.wait()
 
 
@@ -602,14 +647,16 @@
     vm = pltpu.VMEM
     plane = (2, 2, nx, nz)
     padded = (rows + 2 * ny, nz)
+    arrays = (
+        loc, gain, mark, exported, pos, temp.reshape(rows, nz), kappa.reshape(rows, nz), acted, other, gap, snapped
+    )
     temp_new, force = pl.pallas_call(
         functools.partial(kernel, cuts, crosses),
         out_shape=(shape((rows, nz), f32), shape((3 * hi_rows, LANES), f32)),
-        in_specs=[VMEM] * 3 + [ANY] * 2 + [VMEM] * 6,
+        in_specs=[ANY] * 11,
         out_specs=(ANY, VMEM),
-        scratch_shapes=[
-            vm((rows, nz), f32),
-            vm((rows, nz), f32),
+        scratch_shapes=[vm(a.shape, a.dtype) for a in arrays]
+        + [
             vm((rows, nz), f32),
             vm((2 * crosses, 2 * per, LANES), f32),
             vm((crosses, 2 * per, LANES), f32),
@@ -648,23 +695,32 @@
             dma((12,)),
             dma((4,)),
             dma((4,)),
-            dma((4,)),
-            dma((4,)),
+            dma((2,)),
+            dma((2,)),
+            dma((8,)),
+            dma((8,)),
             dma((crosses,)),
             dma((crosses,)),
             dma((2,)),
             dma((2,)),
-            dma((3,)),
+            dma((12,)),
         ],
         compiler_params=pltpu.CompilerParams(collective_id=0, has_side_effects=True),
         name="substeps",
-    )(loc, gain, mark, temp.reshape(rows, nz), kappa.reshape(rows, nz), pos, acted, other, gap, snapped, exported)
+    )(*arrays)
     temp_new, pos_new, vel_new = pl.pallas_call(
         update_kernel,
         out_shape=(shape((rows, nz), f32), shape(pos.shape, f32), shape(vel.shape, f32)),
-        in_specs=[ANY] + [VMEM] * 3,
-        out_specs=(ANY, VMEM, VMEM),
-        scratch_shapes=[vm((4, rows // 4, nz), f32), dma((2, 4))],
+        in_specs=[ANY] * 4,
+        out_specs=(ANY,) * 3,
+        scratch_shapes=[
+            vm((4, rows // 4, nz), f32),
+            vm(force.shape, f32),
+            vm(pos.shape, f32),
+            vm(vel.shape, f32),
+            dma((2, 4)),
+            dma((5,)),
+        ],
         name="update",
     )(temp_new, force, pos, vel)
     return temp_new.reshape(nx, ny, nz), pos_new, vel_new

time: 72.9 us -> 70.8 us (0.971)
  Pallas kernels: 72 us -> 69.4 us
    pallas_call x1, Pallas kernels: 68.5 us -> 67.1 us  [per_device(): pl.pallas_call(functools.partial(kernel, cuts, crosses), out_shape=(shape...]
    pallas_call x1, Pallas kernels: 3.53 us -> 2.29 us  [per_device(): pl.pallas_call(update_kernel, out_shape=(shape((rows, nz), f32), shape(po...]
where the time goes in v4:
time: 70.8 us; the launch traced here: 70 us
  Pallas kernels  69.4 us (98%)
    pallas_call x1, Pallas kernels, per_device(): pl.pallas_call(functools.partial(kernel, cuts, crosses), out_shape=(shape...  67.1 us
    pallas_call x1, Pallas kernels, per_device(): pl.pallas_call(update_kernel, out_shape=(shape((rows, nz), f32), shape(po...  2.29 us

profile of v4, /device:TPU:0, one launch (start us, length us, event | category | flops | bytes accessed | tf_op | source)
XLA Modules:
  0.0 70.0 jit_solution(873141886805468081)
XLA Ops:
  0.6 67.1 %substeps.1 = (f32[2048,128]{1,0:T(8,128)}, f32[96,128]{1,0:T(8,128)}) custom-call(s32[32,128]{1,0:T(8,128)} %bitcast.17, f32[32,128]{1,0:T(8,128)} %bitcast.18, s32[32,128]{1,0:T(8,128)} %bitcast.19, s32[2,128]{1,0:T(2,128)} %bitcast.20, f32[3,4096]{1,0:T(4,128)} %pos_hbm.1, f32[2048,128]{1,0:T(8,128)} %bitcast.11, f32[2048,128]{1,0:T(8,128)} %bitcast.12, ...), custom_call_target="tpu_custom_call" | custom-call | tf_op jit(solution)/shard_map/substeps/pallas_call | solution.py:653
  67.7 2.3 %update.1 = (f32[2048,128]{1,0:T(8,128)}, f32[3,4096]{1,0:T(4,128)}, f32[3,4096]{1,0:T(4,128)}) custom-call(f32[2048,128]{1,0:T(8,128)} %get-tuple-element.8.temp, f32[96,128]{1,0:T(8,128)} %get-tuple-element.9.force_hbm, f32[3,4096]{1,0:T(4,128)} %pos_hbm.1, f32[3,4096]{1,0:T(4,128)} %vel_hbm.1), custom_call_target="tpu_custom_call" | custom-call | tf_op jit(solution)/shard_map/update/pallas_call | solution.py:711

commit v5 on v4

--- a/solution.py
+++ b/solution.py
@@ -117,32 +117,56 @@
     gcount = exported.shape[0]
     bond_rows = acted.shape[0]
 
-    for load in loads[:5]:
+    for load in loads[:3]:
         load.wait()
     w = loc[...].astype(f32)
     power = mark[...].astype(f32) * gain[...] * 0.5
     for j in range(crosses):
         send_lists[j, 0:per, :] = w[j * per : (j + 1) * per]
         send_lists[j, per : 2 * per, :] = power[j * per : (j + 1) * per]
-    e8 = jnp.concatenate([exported[...]] * (8 // gcount), axis=0)
-    eh, el = e8 // LANES, e8 % LANES
-    zero8 = jnp.zeros((8, LANES), f32)
-
-    def row_of(ref, ch, r):
-        return ref[ch : ch + 1, pl.ds(pl.multiple_of(r * LANES, LANES), LANES)]
-
-    def export_rows(r, acc):
-        return tuple(table_pick([(r, row_of(pos, ch, r))], eh, el, acc[ch]) for ch in range(3))
-
-    acc = lax.fori_loop(0, hi_rows, export_rows, (zero8,) * 3, unroll=8)
-    for ch in range(3):
-        gsend[ch * gcount : (ch + 1) * gcount, :] = acc[ch][:gcount]
-
-    for load in loads[5:]:
+    await_all(crosses)
+
+    def send_same(k, carry):
+        j = lax.rem(s + k, crosses)
+        remote(send_lists.at[j], lists.at[s], send_sem.at[j], recv_sem.at[s], (c, j)).start()
+        return carry
+
+    lax.fori_loop(1, crosses, send_same, 0)
+    lists[pl.ds(s, 1)] = send_lists[pl.ds(s, 1)]
+    for load in loads[3:]:
         load.wait()
     for a, ref in enumerate((temp, kappa)):
         ysend0[a, 0] = ref[pl.ds(0, nx, stride=ny), :]
         ysend0[a, 1] = ref[pl.ds(ny - 1, nx, stride=ny), :]
+    early = []
+    for a, ref in enumerate((temp, kappa)):
+        early.append(remote(ysend0.at[a, 1], hy.at[a, 0], hsend.at[4 * a + 2], hrecv.at[4 * a + 2], (c, right)))
+        early.append(remote(ysend0.at[a, 0], hy.at[a, 1], hsend.at[4 * a + 3], hrecv.at[4 * a + 3], (c, left)))
+        early.append(remote(ref.at[pl.ds(rows - ny, ny)], hx.at[a, 0], hsend.at[4 * a], hrecv.at[4 * a], (above, s)))
+        early.append(remote(ref.at[pl.ds(0, ny)], hx.at[a, 1], hsend.at[4 * a + 1], hrecv.at[4 * a + 1], (below, s)))
+    for copy in early:
+        copy.start()
+    e8 = jnp.concatenate([exported[...]] * (8 // gcount), axis=0)
+    eh, el = e8 // LANES, e8 % LANES
+    zero8 = jnp.zeros((8, LANES), f32)
+
+    def row_of(ref, ch, r):
+        return ref[ch : ch + 1, pl.ds(pl.multiple_of(r * LANES, LANES), LANES)]
+
+    def export_rows(r, acc):
+        return tuple(table_pick([(r, row_of(pos, ch, r))], eh, el, acc[ch]) for ch in range(3))
+
+    acc = lax.fori_loop(0, hi_rows, export_rows, (zero8,) * 3, unroll=8)
+    for ch in range(3):
+        gsend[ch * gcount : (ch + 1) * gcount, :] = acc[ch][:gcount]
+
+    late = [
+        remote(gsend, ghosts.at[0], hsend.at[8], hrecv.at[8], (above, s)),
+        remote(gsend, ghosts.at[1], hsend.at[9], hrecv.at[9], (below, s)),
+    ]
+    for copy in late:
+        copy.start()
+    early += late
 
     group = 16
 
@@ -167,26 +191,6 @@
                 pq[ch, pl.ds(pl.multiple_of(k * group + 8 * n, 8), 8), :] = second - first
         return carry
 
-    await_all(crosses)
-
-    def send_same(k, carry):
-        j = lax.rem(s + k, crosses)
-        remote(send_lists.at[j], lists.at[s], send_sem.at[j], recv_sem.at[s], (c, j)).start()
-        return carry
-
-    lax.fori_loop(1, crosses, send_same, 0)
-    lists[pl.ds(s, 1)] = send_lists[pl.ds(s, 1)]
-    early = []
-    for a, ref in enumerate((temp, kappa)):
-        early.append(remote(ysend0.at[a, 1], hy.at[a, 0], hsend.at[4 * a + 2], hrecv.at[4 * a + 2], (c, right)))
-        early.append(remote(ysend0.at[a, 0], hy.at[a, 1], hsend.at[4 * a + 3], hrecv.at[4 * a + 3], (c, left)))
-        early.append(remote(ref.at[pl.ds(rows - ny, ny)], hx.at[a, 0], hsend.at[4 * a], hrecv.at[4 * a], (above, s)))
-        early.append(remote(ref.at[pl.ds(0, ny)], hx.at[a, 1], hsend.at[4 * a + 1], hrecv.at[4 * a + 1], (below, s)))
-    early.append(remote(gsend, ghosts.at[0], hsend.at[8], hrecv.at[8], (above, s)))
-    early.append(remote(gsend, ghosts.at[1], hsend.at[9], hrecv.at[9], (below, s)))
-    for copy in early:
-        copy.start()
-
     block = 16 * ny
 
     def begin(b, carry):
@@ -210,6 +214,7 @@
         return carry
 
     lax.fori_loop(0, bond_rows // 4, lows, 0)
+    lax.fori_loop(0, bond_rows // group // 2, differences, 0)
 
     def take_same(k, carry):
         j = lax.rem(s + k, crosses)
@@ -303,7 +308,7 @@
             c0 = cref[pl.ds(at, nx, stride=ny), :]
             flux[n] = (cc + c0) * ((t0 - t) if n == 0 else (t - t0))
 
-    many = 16
+    many = 32
 
     def step(tin, cin, emit, parts=1, done=None):
 
@@ -316,13 +321,14 @@
                 t1, c1 = tin[ahead, :], cin[ahead, :]
                 fx = (c0 + c1) * (t1 - t0)
                 at = pl.ds(x, 1)
-                ahead_t, ahead_c = pltpu.roll(t0, ny - 1, 0), pltpu.roll(c0, ny - 1, 0)
-                fy = jnp.where(sub == ny - 1, flux[1, at, :], (c0 + ahead_c) * (ahead_t - t0))
-                fy0 = jnp.where(sub == 0, flux[0, at, :], pltpu.roll(fy, 1, 0))
+                north, south = pl.ds(x * ny + ny + 1, ny), pl.ds(x * ny + ny - 1, ny)
+                fy = jnp.where(sub == ny - 1, flux[1, at, :], (c0 + cin[north, :]) * (tin[north, :] - t0))
+                fy0 = jnp.where(sub == 0, flux[0, at, :], (c0 + cin[south, :]) * (t0 - tin[south, :]))
                 ct = c0 * t0
                 tz, cz = pltpu.roll(t0, LANES - 1, 1), pltpu.roll(c0, LANES - 1, 1)
+                tw, cw = pltpu.roll(t0, 1, 1), pltpu.roll(c0, 1, 1)
                 fz = jnp.where(lane == LANES - 1, -ct, (c0 + cz) * (tz - t0))
-                fz0 = jnp.where(lane == 0, ct, pltpu.roll(fz, 1, 1))
+                fz0 = jnp.where(lane == 0, ct, (c0 + cw) * (t0 - tw))
                 emit(x, t0 + 0.5 * (((fx - before) + (fy - fy0)) + (fz - fz0)))
                 before = fx
             return before
@@ -394,14 +400,16 @@
     lax.fori_loop(0, rows // block, finish, 0)
     first += send_x(0, tb)
 
-    lax.fori_loop(0, bond_rows // group // 2, differences, 0)
+    lax.fori_loop(bond_rows // group // 2, bond_rows // group, differences, 0)
     iota32 = iota[:hi_rows]
+
+    turn = 32
 
     def scatter(values):
         def body(k, acc):
             lhs = []
-            for u in range(depth):
-                r = k * depth + u
+            for u in range(turn):
+                r = k * turn + u
                 h = (acted[pl.ds(r, 1), :] // LANES).astype(f32)
                 tops, bottoms = [], []
                 for v in values(r):
@@ -409,13 +417,13 @@
                     tops.append(spread(h, top, iota32))
                     bottoms.append(spread(h, v - top, iota32))
                 lhs.append(jnp.concatenate(tops + bottoms, axis=0))
-            where = pl.ds(pl.multiple_of(k * (depth * LANES), depth * LANES), depth * LANES)
+            where = pl.ds(pl.multiple_of(k * (turn * LANES), turn * LANES), turn * LANES)
             return acc + lax.dot_general(
                 jnp.concatenate(lhs, axis=1), ohl[:, where], NT, preferred_element_type=f32
             )
 
         n = 3 * hi_rows
-        acc = lax.fori_loop(0, bond_rows // depth, body, jnp.zeros((2 * n, LANES), f32))
+        acc = lax.fori_loop(0, bond_rows // turn, body, jnp.zeros((2 * n, LANES), f32))
         return acc[:n] + acc[n:]
 
     def rows_of(lo):
@@ -452,7 +460,6 @@
 
     step(tb, cb, emit_second, pieces, strip_done)
     second = send_x(1, ta)
-    lax.fori_loop(bond_rows // group // 2, bond_rows // group, differences, 0)
     extra_rows = [(hi_rows + side * gcount + g, side, g) for side in range(2) for g in range(gcount)]
     for k in range(0, bond_rows, 8):
         q = other[k : k + 8, :]
@@ -470,6 +477,7 @@
     for ch in range(3):
         pq[ch] = p * d[ch]
         pq[3 + ch] = q * d[ch]
+    own[0] = scatter(rows_of(0))
     for copy in second:
         copy.wait()
 
@@ -524,8 +532,14 @@
     hand = remote(picked.at[pl.ds(crosses, crosses)], far, hsend.at[11], hrecv.at[11], (below, s))
     hand.start()
 
+    chips_y = crosses // 4
+
     def pair(k):
-        return lax.rem(s + 2 * k + 1, crosses), lax.rem(s + 2 * k + 2, crosses)
+        far_x = 1 - k // chips_y
+        y = lax.rem(s // 4 + lax.rem(k, chips_y) + 1, chips_y)
+        x = lax.rem(lax.rem(s // 2, 2) + far_x, 2)
+        chip = 4 * y + 2 * x
+        return chip + 1 - lax.rem(s, 2), chip + lax.rem(s, 2)
 
     def merge(j):
         m = row[pl.ds(j * per, per), :] < 0
@@ -544,11 +558,13 @@
     lax.fori_loop(0, held, look_first, 0)
     hand.wait()
 
-    def send_held(i, carry):
-        back_to(lax.rem(s + i, crosses))
-        return carry
-
-    lax.fori_loop(1, 2 * held + 1, send_held, 0)
+    def send_held(k, carry):
+        a, b = pair(k)
+        back_to(a)
+        back_to(b)
+        return carry
+
+    lax.fori_loop(0, held, send_held, 0)
 
     def look_then(k, carry):
         a, b = pair(k)
@@ -562,7 +578,6 @@
     look((a, b))
     back_to(a)
     back[pl.ds(s, 1)] = merge(s).reshape(1, per, LANES)
-    own[0] = scatter(rows_of(0))
 
     def back_same(k, carry):
         j = lax.rem(s + k, crosses)

time: 70.8 us -> 67.8 us (0.958)
  Pallas kernels: 69.4 us -> 67 us
    pallas_call x1, Pallas kernels: 67.1 us -> 64.7 us  [per_device(): pl.pallas_call(functools.partial(kernel, cuts, crosses), out_shape=(shape...]
where the time goes in v5:
time: 67.8 us; the launch traced here: 67.6 us
  Pallas kernels  67 us (99%)
    pallas_call x1, Pallas kernels, per_device(): pl.pallas_call(functools.partial(kernel, cuts, crosses), out_shape=(shape...  64.7 us
    pallas_call x1, Pallas kernels, per_device(): pl.pallas_call(update_kernel, out_shape=(shape((rows, nz), f32), shape(po...  2.29 us

profile of v5, /device:TPU:0, one launch (start us, length us, event | category | flops | bytes accessed | tf_op | source)
XLA Modules:
  0.0 67.6 jit_solution(16815089927447542348)
XLA Ops:
  0.6 64.7 %substeps.1 = (f32[2048,128]{1,0:T(8,128)}, f32[96,128]{1,0:T(8,128)}) custom-call(s32[32,128]{1,0:T(8,128)} %bitcast.17, f32[32,128]{1,0:T(8,128)} %bitcast.18, s32[32,128]{1,0:T(8,128)} %bitcast.19, s32[2,128]{1,0:T(2,128)} %bitcast.20, f32[3,4096]{1,0:T(4,128)} %pos_hbm.1, f32[2048,128]{1,0:T(8,128)} %bitcast.11, f32[2048,128]{1,0:T(8,128)} %bitcast.12, ...), custom_call_target="tpu_custom_call" | custom-call | tf_op jit(solution)/shard_map/substeps/pallas_call | solution.py:668
  65.3 2.3 %update.1 = (f32[2048,128]{1,0:T(8,128)}, f32[3,4096]{1,0:T(4,128)}, f32[3,4096]{1,0:T(4,128)}) custom-call(f32[2048,128]{1,0:T(8,128)} %get-tuple-element.8.temp, f32[96,128]{1,0:T(8,128)} %get-tuple-element.9.force_hbm, f32[3,4096]{1,0:T(4,128)} %pos_hbm.1, f32[3,4096]{1,0:T(4,128)} %vel_hbm.1), custom_call_target="tpu_custom_call" | custom-call | tf_op jit(solution)/shard_map/update/pallas_call | solution.py:726

commit v6 on v5

--- a/solution.py
+++ b/solution.py
@@ -126,12 +126,26 @@
         send_lists[j, per : 2 * per, :] = power[j * per : (j + 1) * per]
     await_all(crosses)
 
+    chips_y = crosses // 4
+
+    def pair(k):
+        far_x = 1 - k // chips_y
+        y = lax.rem(s // 4 + lax.rem(k, chips_y) + 1, chips_y)
+        x = lax.rem(lax.rem(s // 2, 2) + far_x, 2)
+        chip = 4 * y + 2 * x
+        return chip + 1 - lax.rem(s, 2), chip + lax.rem(s, 2)
+
+    def send_to(j):
+        remote(send_lists.at[j], lists.at[s], send_sem.at[j], recv_sem.at[s], (c, j)).start()
+
     def send_same(k, carry):
-        j = lax.rem(s + k, crosses)
-        remote(send_lists.at[j], lists.at[s], send_sem.at[j], recv_sem.at[s], (c, j)).start()
-        return carry
-
-    lax.fori_loop(1, crosses, send_same, 0)
+        a, b = pair(k)
+        send_to(a)
+        send_to(b)
+        return carry
+
+    lax.fori_loop(0, crosses // 2 - 1, send_same, 0)
+    send_to(pair(crosses // 2 - 1)[0])
     lists[pl.ds(s, 1)] = send_lists[pl.ds(s, 1)]
     for load in loads[3:]:
         load.wait()
@@ -300,21 +314,26 @@
         cref[0:ny, :] = hx[1, 0] * conduct(tref[0:ny, :])
         cref[rows + ny : rows + 2 * ny, :] = hx[1, 1] * conduct(tref[rows + ny : rows + 2 * ny, :])
 
-    def rim(tlo, thi, tref, cref):
-        for n, (off, plane, k, at) in enumerate(((low_edge, tlo, hy[1, 0], ny), (high_edge, thi, hy[1, 1], 2 * ny - 1))):
-            t = jnp.where(off, 0.0, plane)
-            cc = jnp.where(off, 0.0, k) * conduct(t)
-            t0 = tref[pl.ds(at, nx, stride=ny), :]
-            c0 = cref[pl.ds(at, nx, stride=ny), :]
-            flux[n] = (cc + c0) * ((t0 - t) if n == 0 else (t - t0))
+    def rim(planes, tref, cref, start=0, size=nx):
+        part = pl.ds(start, size)
+        for n, (off, at) in enumerate(((low_edge, ny), (high_edge, 2 * ny - 1))):
+            t = jnp.where(off, 0.0, planes[n, part, :])
+            cc = jnp.where(off, 0.0, hy[1, n, part, :]) * conduct(t)
+            here = pl.ds(start * ny + at, size, stride=ny)
+            t0 = tref[here, :]
+            c0 = cref[here, :]
+            flux[n, part, :] = (cc + c0) * ((t0 - t) if n == 0 else (t - t0))
 
     many = 32
-
-    def step(tin, cin, emit, parts=1, done=None):
-
-        def body(b, before):
+    pieces = nx // many
+
+    def step(tin, cin, emit, done=None):
+        def piece(k, carry):
+            first = k * (many * ny)
+            at0, at1 = pl.ds(pl.multiple_of(first, ny), ny), pl.ds(pl.multiple_of(first + ny, ny), ny)
+            before = (cin[at0, :] + cin[at1, :]) * (tin[at1, :] - tin[at0, :])
             for u in range(many):
-                x = b * many + u
+                x = k * many + u
                 here = pl.ds(pl.multiple_of(x * ny + ny, ny), ny)
                 ahead = pl.ds(pl.multiple_of(x * ny + 2 * ny, ny), ny)
                 t0, c0 = tin[here, :], cin[here, :]
@@ -331,21 +350,17 @@
                 fz0 = jnp.where(lane == 0, ct, (c0 + cw) * (t0 - tw))
                 emit(x, t0 + 0.5 * (((fx - before) + (fy - fy0)) + (fz - fz0)))
                 before = fx
-            return before
-
-        t0, c0 = tin[ny : 2 * ny, :], cin[ny : 2 * ny, :]
-        tm, cm = tin[0:ny, :], cin[0:ny, :]
-        turns = nx // many // parts
-
-        def piece(k, before):
-            before = lax.fori_loop(k * turns, (k + 1) * turns, body, before)
-            done(k)
-            return before
-
-        if done is None:
-            lax.fori_loop(0, turns, body, (cm + c0) * (t0 - tm))
-        else:
-            lax.fori_loop(0, parts, piece, (cm + c0) * (t0 - tm))
+            if done is not None:
+                done(k)
+            return carry
+
+        return piece
+
+    def inside(piece):
+        lax.fori_loop(1, pieces - 1, piece, 0)
+
+    def outside(piece):
+        lax.fori_loop(0, 2, lambda n, carry: piece(n * (pieces - 1), carry), 0)
 
     def send_x(k, tref):
         copies = [
@@ -370,12 +385,12 @@
     ta[0:ny, :] = hx[0, 0]
     ta[rows + ny : rows + 2 * ny, :] = hx[0, 1]
     edge(ca, ta)
-    rim(hy[0, 0], hy[0, 1], ta, ca)
+    rim(hy.at[0], ta, ca)
 
     def emit_first(x, t):
         d1[pl.ds(pl.multiple_of(x * ny, ny), ny), :] = t
 
-    step(ta, ca, emit_first)
+    lax.fori_loop(0, pieces, step(ta, ca, emit_first), 0)
     for n, y in enumerate((0, ny - 1)):
         ysend[0, n] = d1[pl.ds(y, nx, stride=ny), :] + src[pl.ds(y, nx, stride=ny), :]
     first = send_y()
@@ -398,7 +413,7 @@
         return carry
 
     lax.fori_loop(0, rows // block, finish, 0)
-    first += send_x(0, tb)
+    sides = send_x(0, tb)
 
     lax.fori_loop(bond_rows // group // 2, bond_rows // group, differences, 0)
     iota32 = iota[:hi_rows]
@@ -429,11 +444,6 @@
     def rows_of(lo):
         return lambda r: [pq[lo + ch, pl.ds(r, 1), :] for ch in range(3)]
 
-    for copy in first:
-        copy.wait()
-    edge(cb, tb)
-    rim(stage[0, 0], stage[0, 1], tb, cb)
-
     def emit_second(x, t):
         where = pl.ds(pl.multiple_of(x * ny, ny), ny)
         here = pl.ds(pl.multiple_of(x * ny + ny, ny), ny)
@@ -441,7 +451,6 @@
         ta[here, :] = t
         ca[here, :] = kappa[where, :] * conduct(t)
 
-    pieces = 4
     width = nx // pieces
 
     def strip(k):
@@ -458,7 +467,15 @@
         for copy in strip(k):
             copy.start()
 
-    step(tb, cb, emit_second, pieces, strip_done)
+    for copy in first:
+        copy.wait()
+    rim(stage.at[0], tb, cb)
+    second_step = step(tb, cb, emit_second, strip_done)
+    inside(second_step)
+    for copy in sides:
+        copy.wait()
+    edge(cb, tb)
+    outside(second_step)
     second = send_x(1, ta)
     extra_rows = [(hi_rows + side * gcount + g, side, g) for side in range(2) for g in range(gcount)]
     for k in range(0, bond_rows, 8):
@@ -478,23 +495,25 @@
         pq[ch] = p * d[ch]
         pq[3 + ch] = q * d[ch]
     own[0] = scatter(rows_of(0))
-    for copy in second:
-        copy.wait()
 
     def strip_taken(k, carry):
         for copy in strip(k):
             copy.wait()
-        return carry
-
-    lax.fori_loop(0, pieces, strip_taken, 0)
-    edge(ca, ta)
-    rim(stage[1, 0], stage[1, 1], ta, ca)
+        rim(stage.at[1], ta, ca, k * width, width)
+        return carry
 
     def emit_third(x, t):
         where = pl.ds(pl.multiple_of(x * ny, ny), ny)
         temp_out[where, :] = t + src[where, :]
 
-    step(ta, ca, emit_third)
+    third_step = step(ta, ca, emit_third)
+    lax.fori_loop(1, pieces - 1, strip_taken, 0)
+    inside(third_step)
+    for copy in second:
+        copy.wait()
+    edge(ca, ta)
+    lax.fori_loop(0, 2, lambda n, carry: strip_taken(n * (pieces - 1), carry), 0)
+    outside(third_step)
     store = pltpu.make_async_copy(temp_out, temp_hbm_out, local.at[11])
     store.start()
 
@@ -531,15 +550,6 @@
     lax.fori_loop(0, crosses // 2, look_below, 0)
     hand = remote(picked.at[pl.ds(crosses, crosses)], far, hsend.at[11], hrecv.at[11], (below, s))
     hand.start()
-
-    chips_y = crosses // 4
-
-    def pair(k):
-        far_x = 1 - k // chips_y
-        y = lax.rem(s // 4 + lax.rem(k, chips_y) + 1, chips_y)
-        x = lax.rem(lax.rem(s // 2, 2) + far_x, 2)
-        chip = 4 * y + 2 * x
-        return chip + 1 - lax.rem(s, 2), chip + lax.rem(s, 2)
 
     def merge(j):
         m = row[pl.ds(j * per, per), :] < 0

time: 67.8 us -> 66.2 us (0.976)
  Pallas kernels: 67 us -> 65.4 us
    pallas_call x1, Pallas kernels: 64.7 us -> 63.1 us  [per_device(): pl.pallas_call(functools.partial(kernel, cuts, crosses), out_shape=(shape...]
where the time goes in v6:
time: 66.2 us; the launch traced here: 66 us
  Pallas kernels  65.4 us (99%)
    pallas_call x1, Pallas kernels, per_device(): pl.pallas_call(functools.partial(kernel, cuts, crosses), out_shape=(shape...  63.1 us
    pallas_call x1, Pallas kernels, per_device(): pl.pallas_call(update_kernel, out_shape=(shape((rows, nz), f32), shape(po...  2.29 us

profile of v6, /device:TPU:0, one launch (start us, length us, event | category | flops | bytes accessed | tf_op | source)
XLA Modules:
  0.0 66.0 jit_solution(3238202300427350933)
XLA Ops:
  0.6 63.1 %substeps.1 = (f32[2048,128]{1,0:T(8,128)}, f32[96,128]{1,0:T(8,128)}) custom-call(s32[32,128]{1,0:T(8,128)} %bitcast.17, f32[32,128]{1,0:T(8,128)} %bitcast.18, s32[32,128]{1,0:T(8,128)} %bitcast.19, s32[2,128]{1,0:T(2,128)} %bitcast.20, f32[3,4096]{1,0:T(4,128)} %pos_hbm.1, f32[2048,128]{1,0:T(8,128)} %bitcast.11, f32[2048,128]{1,0:T(8,128)} %bitcast.12, ...), custom_call_target="tpu_custom_call" | custom-call | tf_op jit(solution)/shard_map/substeps/pallas_call | solution.py:678
  63.7 2.3 %update.1 = (f32[2048,128]{1,0:T(8,128)}, f32[3,4096]{1,0:T(4,128)}, f32[3,4096]{1,0:T(4,128)}) custom-call(f32[2048,128]{1,0:T(8,128)} %get-tuple-element.8.temp, f32[96,128]{1,0:T(8,128)} %get-tuple-element.9.force_hbm, f32[3,4096]{1,0:T(4,128)} %pos_hbm.1, f32[3,4096]{1,0:T(4,128)} %vel_hbm.1), custom_call_target="tpu_custom_call" | custom-call | tf_op jit(solution)/shard_map/update/pallas_call | solution.py:736

commit v7 on v6

--- a/solution.py
+++ b/solution.py
@@ -105,9 +105,11 @@
     c, s, below, above = peers(cuts, crosses)
     left, right = lax.rem(s + crosses - 1, crosses), lax.rem(s + 1, crosses)
     loads = [pltpu.make_async_copy(a, b, local.at[n]) for n, (a, b) in enumerate(zip(inputs, refs[13:24]))]
-    for load in loads:
+    for load in loads[:3]:
         load.start()
     greet(cuts, crosses)
+    for load in loads[3:]:
+        load.start()
     rows = temp.shape[0]
     nx = hy.shape[2]
     ny = rows // nx
@@ -415,7 +417,7 @@
     lax.fori_loop(0, rows // block, finish, 0)
     sides = send_x(0, tb)
 
-    lax.fori_loop(bond_rows // group // 2, bond_rows // group, differences, 0)
+    lax.fori_loop(bond_rows // group // 2, bond_rows // group - 1, differences, 0)
     iota32 = iota[:hi_rows]
 
     turn = 32
@@ -477,6 +479,7 @@
     edge(cb, tb)
     outside(second_step)
     second = send_x(1, ta)
+    lax.fori_loop(bond_rows // group - 1, bond_rows // group, differences, 0)
     extra_rows = [(hi_rows + side * gcount + g, side, g) for side in range(2) for g in range(gcount)]
     for k in range(0, bond_rows, 8):
         q = other[k : k + 8, :]
@@ -494,7 +497,6 @@
     for ch in range(3):
         pq[ch] = p * d[ch]
         pq[3 + ch] = q * d[ch]
-    own[0] = scatter(rows_of(0))
 
     def strip_taken(k, carry):
         for copy in strip(k):
@@ -588,6 +590,7 @@
     look((a, b))
     back_to(a)
     back[pl.ds(s, 1)] = merge(s).reshape(1, per, LANES)
+    own[0] = scatter(rows_of(0))
 
     def back_same(k, carry):
         j = lax.rem(s + k, crosses)

time: 66.2 us -> 66.2 us (level)
  no operation moved by 1% of the time
where the time goes in v7:
time: 66.2 us; the launch traced here: 66 us
  Pallas kernels  65.4 us (99%)
    pallas_call x1, Pallas kernels, per_device(): pl.pallas_call(functools.partial(kernel, cuts, crosses), out_shape=(shape...  63.1 us
    pallas_call x1, Pallas kernels, per_device(): pl.pallas_call(update_kernel, out_shape=(shape((rows, nz), f32), shape(po...  2.29 us

profile of v7, /device:TPU:0, one launch (start us, length us, event | category | flops | bytes accessed | tf_op | source)
XLA Modules:
  0.0 66.0 jit_solution(12100485145281581500)
XLA Ops:
  0.6 63.1 %substeps.1 = (f32[2048,128]{1,0:T(8,128)}, f32[96,128]{1,0:T(8,128)}) custom-call(s32[32,128]{1,0:T(8,128)} %bitcast.17, f32[32,128]{1,0:T(8,128)} %bitcast.18, s32[32,128]{1,0:T(8,128)} %bitcast.19, s32[2,128]{1,0:T(2,128)} %bitcast.20, f32[3,4096]{1,0:T(4,128)} %pos_hbm.1, f32[2048,128]{1,0:T(8,128)} %bitcast.11, f32[2048,128]{1,0:T(8,128)} %bitcast.12, ...), custom_call_target="tpu_custom_call" | custom-call | tf_op jit(solution)/shard_map/substeps/pallas_call | solution.py:681
  63.7 2.3 %update.1 = (f32[2048,128]{1,0:T(8,128)}, f32[3,4096]{1,0:T(4,128)}, f32[3,4096]{1,0:T(4,128)}) custom-call(f32[2048,128]{1,0:T(8,128)} %get-tuple-element.8.temp, f32[96,128]{1,0:T(8,128)} %get-tuple-element.9.force_hbm, f32[3,4096]{1,0:T(4,128)} %pos_hbm.1, f32[3,4096]{1,0:T(4,128)} %vel_hbm.1), custom_call_target="tpu_custom_call" | custom-call | tf_op jit(solution)/shard_map/update/pallas_call | solution.py:739
